TPU v7x, 32 devices: a whole 2x2x4 slice. The times are simulated.
32 devices in a mesh: shot: 4 (over y, x), dom: 8 (over z, core).
Axes of the slice: x: 2, y: 2, z: 4, core: 2. Of those that a mesh axis runs over, the one named last changes fastest.
Arguments:
- velocity: float32 [256, 32, 128], P('dom'), may hold values from 1.5 to 3
- noise_field: float32 [256, 32, 128], P('dom'), may hold values from -6 to 6
- step_size: float32 [1], replicated, may hold values from 0.05 to 0.5
- field_prev: float32 [8, 256, 32, 128], P('shot', 'dom'), may hold values from -6 to 6
- field_now: float32 [8, 256, 32, 128], P('shot', 'dom'), may hold values from -6 to 6
- adjoint_next: float32 [8, 256, 32, 128], P('shot', 'dom'), may hold values from -6 to 6
- adjoint_now: float32 [8, 256, 32, 128], P('shot', 'dom'), may hold values from -6 to 6
- wavelet: float32 [8, 4], P('shot'), may hold values from -8 to 8
- source_cells: int32 [8, 8], P('shot'), may hold values from 0 to 1048575
- source_signs: int32 [8, 8], P('shot'), may hold values from 0 to 1
- record_cells: int32 [8, 256], P('shot'), may hold values from 0 to 1048575
- observed: float32 [8, 4, 256], P('shot'), may hold values from -6 to 6
Outputs:
- new_velocity: float32 [256, 32, 128], P('dom', None, 'shot')
Inputs may be any that keep to these rules, and one draw needn't show every extreme that they name: `source_signs`: 0 stands for a negative sign, 1 for a positive one. `source_cells`: cells flattened as x 32 * 128 + z * 128 + y. `record_cells`: cells flattened as x 32 * 128 + z * 128 + y.
All inputs are finite; a program needn't handle non-finite values.
Results may differ from a plain program's by a relative error of at most 0.00009.
Values sent between devices are 32-bit elements; how exact they have to be, the bound alone decides.
A program may use at most 128 MiB of HBM per device.

v0:
```python
import math

import jax
import jax.numpy as jnp
from jax import lax
from jax.sharding import PartitionSpec as P

STEPS = 4


COEFFS = (-205.0 / 72.0, 8.0 / 5.0, -1.0 / 5.0, 8.0 / 315.0, -1.0 / 560.0)
COURANT = 0.02


def extended(block, sides, width):
    for axis, dim in sides:
        count = lax.axis_size(axis)
        forward = [(i, i + 1) for i in range(count - 1)]
        backward = [(target, source) for source, target in forward]
        low = lax.ppermute(
            lax.slice_in_dim(block, block.shape[dim] - width, None, axis=dim), axis, forward
        )
        high = lax.ppermute(lax.slice_in_dim(block, 0, width, axis=dim), axis, backward)
        block = jnp.concatenate([low, block, high], axis=dim)
    return block


def stencil(padded):
    margin = 4
    rank = padded.ndim
    lengths = [padded.shape[rank - 3 + place] - 2 * margin for place in range(3)]

    def window(offsets):
        sliced = padded
        for place in range(3):
            begin = margin + offsets[place]
            sliced = lax.slice_in_dim(sliced, begin, begin + lengths[place], axis=rank - 3 + place)
        return sliced

    summed = 3.0 * COEFFS[0] * window((0, 0, 0))
    for distance in range(1, 5):
        beside_all = window((distance, 0, 0)) + window((-distance, 0, 0))
        beside_all = beside_all + window((0, distance, 0)) + window((0, -distance, 0))
        beside_all = beside_all + window((0, 0, distance)) + window((0, 0, -distance))
        summed = summed + COEFFS[distance] * beside_all
    return summed


def cosine_basis(length):
    wave_index = jnp.arange(length, dtype=jnp.int32)[:, None]
    position = jnp.arange(length, dtype=jnp.int32)[None, :]
    phase = wave_index * (2 * position + 1) % (4 * length)
    angle = math.pi / (2.0 * length) * phase.astype(jnp.float32)
    factor = jnp.where(wave_index == 0, math.sqrt(1.0 / length), math.sqrt(2.0 / length)).astype(
        jnp.float32
    )
    return factor * jnp.cos(angle)


def prior_gain(length, cutoff):
    scaled = jnp.arange(length, dtype=jnp.float32) / float(cutoff)
    return 1.0 / jnp.sqrt(1.0 + scaled)


def precondition(gradient, noise_cols, rate):
    length = gradient.shape[0]
    basis = cosine_basis(length)
    spectrum = prior_gain(length, length // 32)[:, None]
    highest = lax.Precision.HIGHEST
    grad_hat = jnp.dot(basis, gradient.reshape(length, -1), precision=highest)
    noise_hat = jnp.dot(basis, noise_cols.reshape(length, -1), precision=highest)
    weights = spectrum * (-0.5 * rate * spectrum * grad_hat + jnp.sqrt(rate) * noise_hat)
    update = lax.dot_general(basis, weights, (((0,), (0,)), ((), ())), precision=highest)
    return update.reshape(gradient.shape)


def widen(padded):
    return jnp.pad(padded, ((0, 0), (0, 0), (4, 4), (4, 4)))


def body(
    velocity,
    noise_field,
    step_size,
    field_prev,
    field_now,
    adjoint_next,
    adjoint_now,
    wavelet,
    source_cells,
    source_signs,
    record_cells,
    observed,
):
    speed_sq = COURANT * velocity * velocity
    shots_here = field_now.shape[0]
    slab_rows = velocity.shape[0]
    plane_cells = velocity.shape[1] * velocity.shape[2]
    slab_cells = slab_rows * plane_cells
    first_row = lax.axis_index("dom") * slab_rows
    offset = first_row * plane_cells
    row_ids = jnp.arange(shots_here, dtype=jnp.int32)[:, None]
    source_local = source_cells - offset
    source_inside = (source_local >= 0) & (source_local < slab_cells)
    source_target = jnp.where(source_inside, source_local, slab_cells)
    record_local = record_cells - offset
    record_inside = (record_local >= 0) & (record_local < slab_cells)
    record_target = jnp.where(record_inside, record_local, slab_cells)
    record_clip = jnp.clip(record_local, 0, slab_cells - 1)
    amplitude = (2 * source_signs - 1).astype(jnp.float32)

    def place(field, target, values):
        flat = field.reshape(shots_here, -1)
        rows_full = jnp.broadcast_to(row_ids, target.shape)
        return flat.at[rows_full, target].add(values, mode="drop").reshape(field.shape)

    summed = jnp.zeros(field_now.shape, jnp.float32)
    prior, current = (field_prev, field_now)
    laplacians = []
    samples = []
    for moment in range(STEPS):
        padded = extended(current, (("dom", 1),), 4)
        spread = stencil(widen(padded))
        laplacians.append(spread)
        advanced = 2.0 * current - prior + speed_sq * spread
        advanced = place(advanced, source_target, amplitude * wavelet[:, moment][:, None])
        samples.append(jnp.take_along_axis(advanced.reshape(shots_here, -1), record_clip, axis=1))
        prior, current = (current, advanced)
    adj_later, adj_current = (adjoint_next, adjoint_now)
    for moment in range(STEPS, 0, -1):
        misfit = samples[moment - 1] - observed[:, moment - 1, :]
        padded = extended(adj_current, (("dom", 1),), 4)
        spread = stencil(widen(padded))
        earlier = 2.0 * adj_current - adj_later + speed_sq * spread
        earlier = place(earlier, record_target, misfit)
        adj_later, adj_current = (adj_current, earlier)
        summed = summed + adj_current * laplacians[moment - 1]
    partial_value = 2.0 * COURANT * velocity * jnp.sum(summed, axis=0)
    rate = step_size[0]
    shot_rows = velocity.shape[2] // lax.axis_size("shot")
    start = lax.axis_index("shot") * shot_rows
    share = lax.psum_scatter(partial_value, "shot", scatter_dimension=2, tiled=True)
    noise_part = lax.dynamic_slice_in_dim(noise_field, start, shot_rows, 2)
    grad_cols, noise_cols = (
        lax.all_to_all(share, "dom", split_axis=2, concat_axis=0, tiled=True),
        lax.all_to_all(noise_part, "dom", split_axis=2, concat_axis=0, tiled=True),
    )
    update = precondition(grad_cols, noise_cols, rate)
    returned = lax.all_to_all(update, "dom", split_axis=0, concat_axis=2, tiled=True)
    result = lax.dynamic_slice_in_dim(velocity, start, shot_rows, 2) + returned
    return result


def solution(mesh):
    placed = (
        P("dom", None, None),
        P("dom", None, None),
        P(),
        P("shot", "dom", None, None),
        P("shot", "dom", None, None),
        P("shot", "dom", None, None),
        P("shot", "dom", None, None),
        P("shot", None),
        P("shot", None),
        P("shot", None),
        P("shot", None),
        P("shot", None, None),
    )
    return jax.shard_map(
        body, mesh=mesh, in_specs=placed, out_specs=P("dom", None, "shot"), check_vma=False
    )
```

profile of v0, /device:TPU:0, one launch (start us, length us, event | category | flops | bytes accessed | tf_op | source)
XLA Modules:
  0.0 462.7 jit_solution(6807435353787999571)
XLA Ops:
  7.5 2.4 collective-permute-start.3
  12.9 5.2 %collective-permute-start.1 = (f32[2,4,32,128]{3,2,1,0:T(8,128)}, f32[2,4,32,128]{3,2,1,0:T(8,128)S(1)}, u32[]{:S(2)}, u32[]{:S(2)}) collective-permute-start(f32[2,4,32,128]{3,2,1,0:T(8,128)} %get-tuple-element.50), channel_id=1, source_target_pairs={{0,1},{1,2},{2,3},{3,4},{4,5},{5,6},{6,7},{8,9},{9,10},{10,11},{11... | collective-permute-start | bytes 393224 | tf_op jit(solution)/shard_map/ppermute | solution.py:20
  24.8 1.9 multiply_multiply_fusion
  28.2 2.4 constant_dynamic-update-slice_fusion.5
  31.7 2.4 select_maximum_fusion.12
  35.6 8.2 %multiply_add_fusion.3 = (f32[2,32,32,128]{3,2,1,0:T(8,128)}, f32[2,32,32,128]{3,2,1,0:T(8,128)}) fusion(f32[2,32,32,128]{3,2,1,0:T(8,128)} %param.17, f32[2,32,32,128]{3,2,1,0:T(8,128)} %param.18, f32[32,32,128]{2,1,0:T(8,128)} %multiply_multiply_fusion, f32[2,40,40,136]{3,2,1,0:T(8,128)S(1)} %select_maximum_fusion.12, f32[2,36,32,128]{3,2,1,0:T(8,128)} %copy-done.23, ...), kind=kLoop, calls=%fused_computation.283 | loop fusion | flops 8650752 | bytes 29884416 | tf_op jit(solution)/shard_map/add | solution.py:125
  43.8 2.0 copy.122
  45.8 1.9 scatter_fusion
  47.8 4.5 collective-permute-start.5
  53.9 2.5 select_maximum_fusion.14
  60.7 2.6 select_maximum_fusion.10
  64.0 22.3 %multiply_add_fusion.2 = (f32[2,32,32,128]{3,2,1,0:T(8,128)}, f32[2,32,32,128]{3,2,1,0:T(8,128)}) fusion(f32[2,32,32,128]{3,2,1,0:T(8,128)} %param.18, f32[2,32,32,128]{3,2,1,0:T(8,128)} %bitcast.183, f32[32,32,128]{2,1,0:T(8,128)} %multiply_multiply_fusion, f32[2,40,40,136]{3,2,1,0:T(8,128)} %select_maximum_fusion.10, ...), kind=kLoop, calls=%fused_computation.282 | loop fusion | flops 8650752 | bytes 29884416 | tf_op jit(solution)/shard_map/add | solution.py:125
  86.3 3.0 copy.121
  89.4 2.4 scatter_fusion.1
  94.8 4.6 collective-permute-start.7
  99.4 7.9 %fusion.70 = f32[2,32,32,128]{3,2,1,0:T(8,128)} fusion(f32[2,40,40,136]{3,2,1,0:T(8,128)S(1)} %select_maximum_fusion.14, f32[2,36,32,128]{3,2,1,0:T(8,128)} %copy-done.22, f32[2,36,32,128]{3,2,1,0:T(8,128)} %constant_dynamic-update-slice_fusion, f32[2,32,32,128]{3,2,1,0:T(8,128)S(1)} %copy-done.18, f32[2,32,32,128]{3,2,1,0:T(8,128)} %param.19, ...), kind=kLoop, calls=%fused_computation.253 | loop fusion | flops 8650752 | bytes 28835840 | tf_op jit(solution)/shard_map/add | solution.py:134
  107.4 3.2 copy.123
  110.6 4.8 %gather_fusion.3 = f32[512]{0:T(512)S(1)} fusion(f32[2,131072]{1,0:T(2,128)S(1)} %copy-done.15, s32[512]{0:T(512)S(1)} %bitcast.159), kind=kCustom, calls=%fused_computation.3.clone | custom fusion | bytes 8192 | tf_op jit(solution)/shard_map/jit(take_along_axis)/gather | solution.py:127
  120.5 2.5 select_maximum_fusion.8
  123.8 8.3 %multiply_add_fusion.1 = (f32[2,32,32,128]{3,2,1,0:T(8,128)}, f32[2,32,32,128]{3,2,1,0:T(8,128)}) fusion(f32[2,32,32,128]{3,2,1,0:T(8,128)} %bitcast.184, f32[2,32,32,128]{3,2,1,0:T(8,128)} %bitcast.187, f32[32,32,128]{2,1,0:T(8,128)} %multiply_multiply_fusion, f32[2,40,40,136]{3,2,1,0:T(8,128)S(1)} %select_maximum_fusion.8, ...), kind=kLoop, calls=%fused_computation.281 | loop fusion | flops 8650752 | bytes 29884416 | tf_op jit(solution)/shard_map/add | solution.py:125
  132.0 2.1 copy.120
  135.6 5.4 %collective-permute-start.9 = (f32[2,4,32,128]{3,2,1,0:T(8,128)S(1)}, f32[2,4,32,128]{3,2,1,0:T(8,128)S(1)}, u32[]{:S(2)}, u32[]{:S(2)}) collective-permute-start(f32[2,4,32,128]{3,2,1,0:T(8,128)S(1)} %get-tuple-element.34), channel_id=1, source_target_pairs={{0,1},{1,2},{2,3},{3,4},{4,5},{5,6},{6,7},{8,9},{9,10},{10,11},{11... | collective-permute-start | bytes 393224 | tf_op jit(solution)/shard_map/ppermute | solution.py:20
  142.4 7.1 %gather_fusion.2 = f32[512]{0:T(512)} fusion(f32[2,131072]{1,0:T(2,128)S(1)} %copy-done.16, s32[512]{0:T(512)S(1)} %bitcast.160), kind=kCustom, calls=%fused_computation.2.clone | custom fusion | bytes 8192 | tf_op jit(solution)/shard_map/jit(take_along_axis)/gather | solution.py:127
  150.1 4.8 %gather_fusion.1 = f32[512]{0:T(512)S(1)} fusion(f32[2,131072]{1,0:T(2,128)S(1)} %scatter_fusion.2, s32[512]{0:T(512)S(1)} %bitcast.161), kind=kCustom, calls=%fused_computation.1.clone | custom fusion | bytes 8192 | tf_op jit(solution)/shard_map/jit(take_along_axis)/gather | solution.py:127
  159.5 2.5 select_maximum_fusion.6
  162.7 8.2 %multiply_add_fusion = (f32[2,32,32,128]{3,2,1,0:T(8,128)}, f32[2,32,32,128]{3,2,1,0:T(8,128)}) fusion(f32[2,32,32,128]{3,2,1,0:T(8,128)} %bitcast.188, f32[2,32,32,128]{3,2,1,0:T(8,128)} %bitcast.199, f32[32,32,128]{2,1,0:T(8,128)} %multiply_multiply_fusion, f32[2,40,40,136]{3,2,1,0:T(8,128)S(1)} %select_maximum_fusion.6, ...), kind=kLoop, calls=%fused_computation.280 | loop fusion | flops 8650752 | bytes 29884416 | tf_op jit(solution)/shard_map/add | solution.py:125
  171.0 2.1 copy.119
  174.4 4.8 %gather_fusion = f32[512]{0:T(512)S(1)} fusion(f32[2,131072]{1,0:T(2,128)S(1)} %scatter_fusion.3, s32[512]{0:T(512)S(1)} %bitcast.162), kind=kCustom, calls=%fused_computation.clone | custom fusion | bytes 8192 | tf_op jit(solution)/shard_map/jit(take_along_axis)/gather | solution.py:127
  179.4 24.7 %scatter_fusion.4 = f32[2,131072]{1,0:T(2,128)S(1)} fusion(f32[2,131072]{1,0:T(2,128)S(1)} %bitcast.200, s32[512]{0:T(512)S(1)} %bitcast.155, f32[512]{0:T(512)S(1)} %bitcast.227), kind=kCustom, calls=%fused_computation.8 | custom fusion | flops 512 | bytes 10240 | tf_op jit(solution)/shard_map/scatter-add | solution.py:115
  204.2 4.3 collective-permute-start.11
  214.2 7.8 %fusion.28 = f32[2,32,32,128]{3,2,1,0:T(8,128)} fusion(f32[2,40,40,136]{3,2,1,0:T(8,128)S(1)} %select_maximum_fusion.4, f32[2,36,32,128]{3,2,1,0:T(8,128)} %copy-done.26, f32[2,36,32,128]{3,2,1,0:T(8,128)} %constant_dynamic-update-slice_fusion.20, f32[2,32,32,128]{3,2,1,0:T(8,128)S(1)} %bitcast.166, f32[2,32,32,128]{3,2,1,0:T(8,128)} %param.20, ...), kind=kLoop, calls=%fused_computation.111 | loop fusion | flops 8650752 | bytes 28835840 | tf_op jit(solution)/shard_map/add | solution.py:134
  222.0 2.0 copy.118
  224.1 24.7 %scatter_fusion.5 = f32[2,131072]{1,0:T(2,128)S(1)} fusion(f32[2,131072]{1,0:T(2,128)S(1)} %bitcast.205, s32[512]{0:T(512)S(1)} %bitcast.156, f32[512]{0:T(512)S(1)} %bitcast.225), kind=kCustom, calls=%fused_computation.9 | custom fusion | flops 512 | bytes 10240 | tf_op jit(solution)/shard_map/scatter-add | solution.py:115
  248.9 4.7 %collective-permute-start.13 = (f32[2,4,32,128]{3,2,1,0:T(8,128)S(1)}, f32[2,4,32,128]{3,2,1,0:T(8,128)S(1)}, u32[]{:S(2)}, u32[]{:S(2)}) collective-permute-start(f32[2,4,32,128]{3,2,1,0:T(8,128)S(1)} %get-tuple-element.26), channel_id=1, source_target_pairs={{0,1},{1,2},{2,3},{3,4},{4,5},{5,6},{6,7},{8,9},{9,10},{10,11},{11... | collective-permute-start | bytes 393224 | tf_op jit(solution)/shard_map/ppermute | solution.py:20
  259.5 7.8 %fusion.18 = f32[2,32,32,128]{3,2,1,0:T(8,128)} fusion(f32[2,40,40,136]{3,2,1,0:T(8,128)S(1)} %select_maximum_fusion.2, f32[2,36,32,128]{3,2,1,0:T(8,128)} %copy-done.27, f32[2,36,32,128]{3,2,1,0:T(8,128)} %constant_dynamic-update-slice_fusion.24, f32[2,32,32,128]{3,2,1,0:T(8,128)} %bitcast.172, f32[2,32,32,128]{3,2,1,0:T(8,128)S(1)} %bitcast.167, ...), kind=kLoop, calls=%fused_computation.81 | loop fusion | flops 8650752 | bytes 28835840 | tf_op jit(solution)/shard_map/add | solution.py:134
  267.2 2.0 copy.117
  269.3 24.7 %scatter_fusion.6 = f32[2,131072]{1,0:T(2,128)S(1)} fusion(f32[2,131072]{1,0:T(2,128)S(1)} %bitcast.207, s32[512]{0:T(512)S(1)} %bitcast.157, f32[512]{0:T(512)S(1)} %bitcast.226), kind=kCustom, calls=%fused_computation.10 | custom fusion | flops 512 | bytes 10240 | tf_op jit(solution)/shard_map/scatter-add | solution.py:115
  294.1 4.7 %collective-permute-start.15 = (f32[2,4,32,128]{3,2,1,0:T(8,128)S(1)}, f32[2,4,32,128]{3,2,1,0:T(8,128)S(1)}, u32[]{:S(2)}, u32[]{:S(2)}) collective-permute-start(f32[2,4,32,128]{3,2,1,0:T(8,128)S(1)} %get-tuple-element.22), channel_id=1, source_target_pairs={{0,1},{1,2},{2,3},{3,4},{4,5},{5,6},{6,7},{8,9},{9,10},{10,11},{11... | collective-permute-start | bytes 393224 | tf_op jit(solution)/shard_map/ppermute | solution.py:20
  304.6 7.9 %fusion.8 = f32[2,32,32,128]{3,2,1,0:T(8,128)} fusion(f32[2,40,40,136]{3,2,1,0:T(8,128)S(1)} %select_maximum_fusion, f32[2,36,32,128]{3,2,1,0:T(8,128)} %copy-done.28, f32[2,36,32,128]{3,2,1,0:T(8,128)} %constant_dynamic-update-slice_fusion.28, f32[2,32,32,128]{3,2,1,0:T(8,128)} %bitcast.178, f32[2,32,32,128]{3,2,1,0:T(8,128)S(1)} %bitcast.173, ...), kind=kLoop, calls=%fused_computation.51 | loop fusion | flops 8650752 | bytes 28835840 | tf_op jit(solution)/shard_map/add | solution.py:134
  312.5 3.0 copy.116
  315.5 70.0 %scatter_fusion.7 = f32[2,131072]{1,0:T(2,128)} fusion(f32[2,131072]{1,0:T(2,128)} %bitcast.203, s32[512]{0:T(512)S(1)} %bitcast.158, f32[512]{0:T(512)S(1)} %bitcast.224), kind=kCustom, calls=%fused_computation.11 | custom fusion | flops 512 | bytes 10240 | tf_op jit(solution)/shard_map/scatter-add | solution.py:115
  386.9 3.3 add_reduce_fusion
  395.7 6.8 %all-to-all-start.1 = ((f32[8,1,4096]{2,1,0:T(1,128)}), f32[8,1,4096]{2,1,0:T(1,128)S(1)}, u32[]{:S(2)}, u32[]{:S(2)}) async-start(f32[8,1,4096]{2,1,0:T(1,128)} %reshape.257), calls=%async_computation.1 | async-start | bytes 262144 | tf_op jit(solution)/shard_map/all_to_all | solution.py:146
  402.5 19.8 %reduce-scatter.4.cloned.1.call-done = f32[32,1024]{1,0:T(8,128)} async-done(((f32[128,1024]{1,0:T(8,128)}), f32[32,1024]{1,0:T(8,128)}) %reduce-scatter.4.cloned.1.call-update) | async-done | bytes 131088
  424.3 4.8 %all-to-all-start = ((f32[8,1,4096]{2,1,0:T(1,128)}), f32[8,1,4096]{2,1,0:T(1,128)S(1)}, u32[]{:S(2)}, u32[]{:S(2)}) async-start(f32[8,1,4096]{2,1,0:T(1,128)} %reshape.255), calls=%async_computation | async-start | bytes 262144 | tf_op jit(solution)/shard_map/all_to_all | solution.py:145
  432.3 3.6 all-to-all-done
  443.0 3.4 all-to-all-start.2
  446.9 6.2 %all-to-all-done.2 = f32[8,1,4096]{2,1,0:T(1,128)S(1)} async-done(((f32[8,1,4096]{2,1,0:T(1,128)}), f32[8,1,4096]{2,1,0:T(1,128)S(1)}, u32[]{:S(2)}, u32[]{:S(2)}) %all-to-all-start.2) | async-done | bytes 131104 | tf_op jit(solution)/shard_map/all_to_all | solution.py:149
  (209 shorter events, 78.6 us)
Async XLA Ops:
  6.5 415.8 %reduce-scatter.4.cloned.1.call-start = ((), (), s32[]{:S(2)}) async-start(), calls=%async_computation.4 | async-start | bytes 655360
  7.5 20.6 %collective-permute-start.3 = (f32[2,4,32,128]{3,2,1,0:T(8,128)S(1)}, f32[2,4,32,128]{3,2,1,0:T(8,128)S(1)}, u32[]{:S(2)}, u32[]{:S(2)}) collective-permute-start(f32[2,4,32,128]{3,2,1,0:T(8,128)S(1)} %get-tuple-element.46), channel_id=1, source_target_pairs={{0,1},{1,2},{2,3},{3,4},{4,5},{5,6},{6,7},{8,9},{9,10},{10,11},{11... | collective-permute-start | bytes 393224 | tf_op jit(solution)/shard_map/ppermute | solution.py:20
  9.9 21.7 %collective-permute-start.2 = (f32[2,4,32,128]{3,2,1,0:T(8,128)S(1)}, f32[2,4,32,128]{3,2,1,0:T(8,128)}, u32[]{:S(2)}, u32[]{:S(2)}) collective-permute-start(f32[2,4,32,128]{3,2,1,0:T(8,128)S(1)} %get-tuple-element.47), channel_id=1, source_target_pairs={{1,0},{2,1},{3,2},{4,3},{5,4},{6,5},{7,6},{9,8},{10,9},{11,10},{12... | collective-permute-start | bytes 393224 | tf_op jit(solution)/shard_map/ppermute | solution.py:23
  12.9 40.9 %collective-permute-start.1 = (f32[2,4,32,128]{3,2,1,0:T(8,128)}, f32[2,4,32,128]{3,2,1,0:T(8,128)S(1)}, u32[]{:S(2)}, u32[]{:S(2)}) collective-permute-start(f32[2,4,32,128]{3,2,1,0:T(8,128)} %get-tuple-element.50), channel_id=1, source_target_pairs={{0,1},{1,2},{2,3},{3,4},{4,5},{5,6},{6,7},{8,9},{9,10},{10,11},{11... | collective-permute-start | bytes 393224 | tf_op jit(solution)/shard_map/ppermute | solution.py:20
  18.1 35.8 %collective-permute-start = (f32[2,4,32,128]{3,2,1,0:T(8,128)}, f32[2,4,32,128]{3,2,1,0:T(8,128)S(1)}, u32[]{:S(2)}, u32[]{:S(2)}) collective-permute-start(f32[2,4,32,128]{3,2,1,0:T(8,128)} %get-tuple-element.51), channel_id=1, source_target_pairs={{1,0},{2,1},{3,2},{4,3},{5,4},{6,5},{7,6},{9,8},{10,9},{11,10},{12... | collective-permute-start | bytes 393224 | tf_op jit(solution)/shard_map/ppermute | solution.py:23
  24.0 7.6 %copy-start.19 = (f32[2,32,32,128]{3,2,1,0:T(8,128)S(1)}, f32[2,32,32,128]{3,2,1,0:T(8,128)}, u32[]{:S(2)}) copy-start(f32[2,32,32,128]{3,2,1,0:T(8,128)} %param.18) | copy-start | bytes 3145732
  47.7 6.2 %copy-start.14 = (f32[2,131072]{1,0:T(2,128)}, f32[2,131072]{1,0:T(2,128)S(1)}, u32[]{:S(2)}) copy-start(f32[2,131072]{1,0:T(2,128)S(1)} %scatter_fusion) | copy-start | bytes 3145732
  47.7 8.7 %copy-start.17 = (f32[2,32,32,128]{3,2,1,0:T(8,128)S(1)}, f32[2,32,32,128]{3,2,1,0:T(8,128)}, u32[]{:S(2)}) copy-start(f32[2,32,32,128]{3,2,1,0:T(8,128)} %param.20) | copy-start | bytes 3145732
  47.8 12.9 %copy-start.11 = (f32[1,2,1024,128]{3,2,1,0:T(8,128)}, f32[1,2,1024,128]{3,2,1,0:T(8,128)S(1)}, u32[]{:S(2)}) copy-start(f32[1,2,1024,128]{3,2,1,0:T(8,128)S(1)} %copy.74) | copy-start | bytes 3145732
  47.8 10.5 %collective-permute-start.5 = (f32[2,4,32,128]{3,2,1,0:T(8,128)S(1)}, f32[2,4,32,128]{3,2,1,0:T(8,128)S(1)}, u32[]{:S(2)}, u32[]{:S(2)}) collective-permute-start(f32[2,4,32,128]{3,2,1,0:T(8,128)S(1)} %get-tuple-element.42), channel_id=1, source_target_pairs={{0,1},{1,2},{2,3},{3,4},{4,5},{5,6},{6,7},{8,9},{9,10},{10,11},{11... | collective-permute-start | bytes 393224 | tf_op jit(solution)/shard_map/ppermute | solution.py:20
  52.4 8.3 %collective-permute-start.4 = (f32[2,4,32,128]{3,2,1,0:T(8,128)S(1)}, f32[2,4,32,128]{3,2,1,0:T(8,128)S(1)}, u32[]{:S(2)}, u32[]{:S(2)}) collective-permute-start(f32[2,4,32,128]{3,2,1,0:T(8,128)S(1)} %get-tuple-element.43), channel_id=1, source_target_pairs={{1,0},{2,1},{3,2},{4,3},{5,4},{6,5},{7,6},{9,8},{10,9},{11,10},{12... | collective-permute-start | bytes 393224 | tf_op jit(solution)/shard_map/ppermute | solution.py:23
  57.6 5.7 %copy-start.22 = (f32[2,36,32,128]{3,2,1,0:T(8,128)}, f32[2,36,32,128]{3,2,1,0:T(8,128)S(1)}, u32[]{:S(2)}) copy-start(f32[2,36,32,128]{3,2,1,0:T(8,128)S(1)} %get-tuple-element.49) | copy-start | bytes 3538948
  91.7 7.7 %copy-start.18 = (f32[2,32,32,128]{3,2,1,0:T(8,128)S(1)}, f32[2,32,32,128]{3,2,1,0:T(8,128)}, u32[]{:S(2)}) copy-start(f32[2,32,32,128]{3,2,1,0:T(8,128)} %param.20) | copy-start | bytes 3145732
  94.8 22.7 %collective-permute-start.7 = (f32[2,4,32,128]{3,2,1,0:T(8,128)}, f32[2,4,32,128]{3,2,1,0:T(8,128)S(1)}, u32[]{:S(2)}, u32[]{:S(2)}) collective-permute-start(f32[2,4,32,128]{3,2,1,0:T(8,128)} %get-tuple-element.38), channel_id=1, source_target_pairs={{0,1},{1,2},{2,3},{3,4},{4,5},{5,6},{6,7},{8,9},{9,10},{10,11},{11... | collective-permute-start | bytes 393224 | tf_op jit(solution)/shard_map/ppermute | solution.py:20
  107.3 10.2 %copy-start.13 = (f32[1,2,1024,128]{3,2,1,0:T(8,128)S(1)}, f32[1,2,1024,128]{3,2,1,0:T(8,128)}, u32[]{:S(2)}) copy-start(f32[1,2,1024,128]{3,2,1,0:T(8,128)} %copy-done.12) | copy-start | bytes 3145732
  116.0 4.6 collective-permute-start.6
  123.8 10.4 %copy-start.41 = (f32[16]{0:T(128)S(1)}, f32[16]{0:T(128)}, u32[]{:S(2)}) copy-start(f32[16]{0:T(128)} %reshape.175) | copy-start | bytes 196
  132.0 9.1 %copy-start.33 = (s32[2,256]{1,0:T(2,128)S(1)}, s32[2,256]{1,0:T(2,128)}, u32[]{:S(2)}) copy-start(s32[2,256]{1,0:T(2,128)} %param.24) | copy-start | bytes 6148
  132.0 10.4 %copy-start.16 = (f32[2,131072]{1,0:T(2,128)S(1)}, f32[2,131072]{1,0:T(2,128)}, u32[]{:S(2)}) copy-start(f32[2,131072]{1,0:T(2,128)} %scatter_fusion.1) | copy-start | bytes 3145732
  135.6 22.8 %copy-start.20 = (f32[1,2,1024,128]{3,2,1,0:T(8,128)}, f32[1,2,1024,128]{3,2,1,0:T(8,128)S(1)}, u32[]{:S(2)}) copy-start(f32[1,2,1024,128]{3,2,1,0:T(8,128)S(1)} %copy.78) | copy-start | bytes 3145732
  135.6 21.6 %collective-permute-start.9 = (f32[2,4,32,128]{3,2,1,0:T(8,128)S(1)}, f32[2,4,32,128]{3,2,1,0:T(8,128)S(1)}, u32[]{:S(2)}, u32[]{:S(2)}) collective-permute-start(f32[2,4,32,128]{3,2,1,0:T(8,128)S(1)} %get-tuple-element.34), channel_id=1, source_target_pairs={{0,1},{1,2},{2,3},{3,4},{4,5},{5,6},{6,7},{8,9},{9,10},{10,11},{11... | collective-permute-start | bytes 393224 | tf_op jit(solution)/shard_map/ppermute | solution.py:20
  155.6 3.9 collective-permute-start.8
  162.7 10.4 %copy-start.40 = (f32[16]{0:T(128)S(1)}, f32[16]{0:T(128)}, u32[]{:S(2)}) copy-start(f32[16]{0:T(128)} %reshape.181) | copy-start | bytes 196
  170.9 8.4 %copy-start.35 = (f32[2,256]{1,0:T(2,128)S(1)}, f32[2,256]{1,0:T(2,128)}, u32[]{:S(2)}) copy-start(f32[2,256]{1,0:T(2,128)} %reshape.238) | copy-start | bytes 6148
  170.9 8.4 %copy-start.36 = (f32[2,1,256]{2,1,0:T(1,128)S(1)}, f32[2,1,256]{2,1,0:T(1,128)}, u32[]{:S(2)}) copy-start(f32[2,1,256]{2,1,0:T(1,128)} %get-tuple-element.52) | copy-start | bytes 6148
  170.9 8.4 %copy-start.37 = (f32[2,1,256]{2,1,0:T(1,128)S(1)}, f32[2,1,256]{2,1,0:T(1,128)}, u32[]{:S(2)}) copy-start(f32[2,1,256]{2,1,0:T(1,128)} %get-tuple-element.53) | copy-start | bytes 6148
  170.9 8.4 %copy-start.38 = (f32[2,1,256]{2,1,0:T(1,128)S(1)}, f32[2,1,256]{2,1,0:T(1,128)}, u32[]{:S(2)}) copy-start(f32[2,1,256]{2,1,0:T(1,128)} %get-tuple-element.55) | copy-start | bytes 6148
  170.9 8.4 %copy-start.39 = (pred[2,256]{1,0:T(4,128)(4,1)S(1)}, pred[2,256]{1,0:T(4,128)(4,1)}, u32[]{:S(2)}) copy-start(pred[2,256]{1,0:T(4,128)(4,1)} %get-tuple-element.11) | copy-start | bytes 1540
  170.9 8.4 %copy-start.21 = (f32[1,2,1024,128]{3,1,2,0:T(2,128)S(1)}, f32[1,2,1024,128]{3,1,2,0:T(2,128)}, u32[]{:S(2)}) copy-start(f32[1,2,1024,128]{3,1,2,0:T(2,128)} %copy.123) | copy-start | bytes 3145732
  204.2 10.0 %copy-start.3 = (f32[1,2,1024,128]{3,2,1,0:T(8,128)}, f32[1,2,1024,128]{3,2,1,0:T(8,128)S(1)}, u32[]{:S(2)}) copy-start(f32[1,2,1024,128]{3,2,1,0:T(8,128)S(1)} %copy.82) | copy-start | bytes 3145732
  204.2 5.6 %collective-permute-start.11 = (f32[2,4,32,128]{3,2,1,0:T(8,128)S(1)}, f32[2,4,32,128]{3,2,1,0:T(8,128)S(1)}, u32[]{:S(2)}, u32[]{:S(2)}) collective-permute-start(f32[2,4,32,128]{3,2,1,0:T(8,128)S(1)} %get-tuple-element.30), channel_id=1, source_target_pairs={{0,1},{1,2},{2,3},{3,4},{4,5},{5,6},{6,7},{8,9},{9,10},{10,11},{11... | collective-permute-start | bytes 393224 | tf_op jit(solution)/shard_map/ppermute | solution.py:20
  208.5 3.5 collective-permute-start.10
  248.9 9.9 %copy-start.6 = (f32[1,2,1024,128]{3,2,1,0:T(8,128)}, f32[1,2,1024,128]{3,2,1,0:T(8,128)S(1)}, u32[]{:S(2)}) copy-start(f32[1,2,1024,128]{3,2,1,0:T(8,128)S(1)} %copy.85) | copy-start | bytes 3145732
  248.9 6.2 %collective-permute-start.13 = (f32[2,4,32,128]{3,2,1,0:T(8,128)S(1)}, f32[2,4,32,128]{3,2,1,0:T(8,128)S(1)}, u32[]{:S(2)}, u32[]{:S(2)}) collective-permute-start(f32[2,4,32,128]{3,2,1,0:T(8,128)S(1)} %get-tuple-element.26), channel_id=1, source_target_pairs={{0,1},{1,2},{2,3},{3,4},{4,5},{5,6},{6,7},{8,9},{9,10},{10,11},{11... | collective-permute-start | bytes 393224 | tf_op jit(solution)/shard_map/ppermute | solution.py:20
  253.6 3.7 collective-permute-start.12
  255.1 4.4 copy-start.1
  255.1 4.4 copy-start.4
  269.3 29.6 %copy-start.34 = (f32[1,2,2,128]{3,2,1,0:T(2,128)S(1)}, f32[1,2,2,128]{3,2,1,0:T(2,128)}, u32[]{:S(2)}) copy-start(f32[1,2,2,128]{3,2,1,0:T(2,128)} %get-tuple-element.10) | copy-start | bytes 6148
  294.1 9.8 %copy-start.9 = (f32[1,2,1024,128]{3,2,1,0:T(8,128)}, f32[1,2,1024,128]{3,2,1,0:T(8,128)S(1)}, u32[]{:S(2)}) copy-start(f32[1,2,1024,128]{3,2,1,0:T(8,128)S(1)} %copy.88) | copy-start | bytes 3145732
  294.1 6.1 %collective-permute-start.15 = (f32[2,4,32,128]{3,2,1,0:T(8,128)S(1)}, f32[2,4,32,128]{3,2,1,0:T(8,128)S(1)}, u32[]{:S(2)}, u32[]{:S(2)}) collective-permute-start(f32[2,4,32,128]{3,2,1,0:T(8,128)S(1)} %get-tuple-element.22), channel_id=1, source_target_pairs={{0,1},{1,2},{2,3},{3,4},{4,5},{5,6},{6,7},{8,9},{9,10},{10,11},{11... | collective-permute-start | bytes 393224 | tf_op jit(solution)/shard_map/ppermute | solution.py:20
  298.9 3.5 collective-permute-start.14
  300.2 4.4 copy-start.2
  315.5 71.3 %copy-start.5 = (f32[1,2,1024,128]{3,2,1,0:T(8,128)S(1)}, f32[1,2,1024,128]{3,2,1,0:T(8,128)}, u32[]{:S(2)}) copy-start(f32[1,2,1024,128]{3,2,1,0:T(8,128)} %copy-done.3) | copy-start | bytes 3145732
  315.5 71.3 %copy-start.8 = (f32[1,2,1024,128]{3,2,1,0:T(8,128)S(1)}, f32[1,2,1024,128]{3,2,1,0:T(8,128)}, u32[]{:S(2)}) copy-start(f32[1,2,1024,128]{3,2,1,0:T(8,128)} %copy-done.6) | copy-start | bytes 3145732
  315.5 71.3 %copy-start.10 = (f32[1,2,1024,128]{3,2,1,0:T(8,128)S(1)}, f32[1,2,1024,128]{3,2,1,0:T(8,128)}, u32[]{:S(2)}) copy-start(f32[1,2,1024,128]{3,2,1,0:T(8,128)} %copy-done.9) | copy-start | bytes 3145732
  395.7 28.6 %all-to-all-start.1 = ((f32[8,1,4096]{2,1,0:T(1,128)}), f32[8,1,4096]{2,1,0:T(1,128)S(1)}, u32[]{:S(2)}, u32[]{:S(2)}) async-start(f32[8,1,4096]{2,1,0:T(1,128)} %reshape.257), calls=%async_computation.1 | async-start | bytes 262144 | tf_op jit(solution)/shard_map/all_to_all | solution.py:146
  424.3 11.5 %all-to-all-start = ((f32[8,1,4096]{2,1,0:T(1,128)}), f32[8,1,4096]{2,1,0:T(1,128)S(1)}, u32[]{:S(2)}, u32[]{:S(2)}) async-start(f32[8,1,4096]{2,1,0:T(1,128)} %reshape.255), calls=%async_computation | async-start | bytes 262144 | tf_op jit(solution)/shard_map/all_to_all | solution.py:145
  443.0 10.1 %all-to-all-start.2 = ((f32[8,1,4096]{2,1,0:T(1,128)}), f32[8,1,4096]{2,1,0:T(1,128)S(1)}, u32[]{:S(2)}, u32[]{:S(2)}) async-start(f32[8,1,4096]{2,1,0:T(1,128)} %reshape.259), calls=%async_computation.2 | async-start | bytes 262144 | tf_op jit(solution)/shard_map/all_to_all | solution.py:149
  (14 other events, 30.4 us)
Sparse Core Ops, SparseCore 0:
  394.1 28.1 reduce-scatter.3
where the time goes:
time: 470 us; the launch traced here: 463 us
  other arithmetic  258 us (55%)
  local copies, waits for them, and re-layouts  92.2 us (20%)
  starting transfers between devices  62.2 us (13%)
  waiting for transfers between devices  30.5 us (6%)
  between operations  15.5 us (3%)
    scatter-add x8, other arithmetic, place(): flat.at[rows_full, target].add(values, mode='drop').reshape(field.shape)  151 us
    unnamed x133, local copies, waits for them, and re-layouts  50.7 us
    add x4, other arithmetic, body(): advanced = 2.0 * current - prior + speed_sq * spread  47 us
    ppermute x8, starting transfers between devices, extended(): lax.ppermute(lax.slice_in_dim(block, block.shape[dim] - width, None, axis...  35.9 us
    add x4, other arithmetic, body(): earlier = 2.0 * adj_current - adj_later + speed_sq * spread  31.4 us
    gather x8, local copies, waits for them, and re-layouts, body(): jnp.take_along_axis(advanced.reshape(shots_here, -1), record_clip, axis=1)  23.5 us
    unnamed x2, waiting for transfers between devices  19.8 us
    concatenate x8, other arithmetic, extended(): block = jnp.concatenate([low, block, high], axis=dim)  16.9 us
  transfers between devices with their start and end apart: 20, of which 4 were waited for; matrix products, arithmetic and copies ran while one was open for 17% of the time, Pallas kernels for 0%

commit v1 on v0

v1 whole, which is shorter than its diff:
```python
import functools
import math

import jax
import jax.numpy as jnp
from jax import lax
from jax.experimental import pallas as pl
from jax.experimental.pallas import tpu as pltpu
from jax.sharding import PartitionSpec as P

STEPS = 4


COEFFS = (-205.0 / 72.0, 8.0 / 5.0, -1.0 / 5.0, 8.0 / 315.0, -1.0 / 560.0)
COURANT = 0.02


MARGIN = 4
MESH = pl.DeviceIdType.MESH


def split_two(value):
    high = value.astype(jnp.bfloat16)
    low = (value - high.astype(jnp.float32)).astype(jnp.bfloat16)
    return jnp.concatenate([high, low], axis=-1)


def wave_kernel(
    doms,
    now_hbm,
    adj_hbm,
    prev_hbm,
    later_hbm,
    speed_hbm,
    pulse,
    rec_col,
    rec_lane,
    src_col,
    src_lane,
    signs,
    observed,
    out,
    ext,
    prev,
    later,
    speed,
    laps,
    spread_src,
    landed,
    pick,
    put,
    hot,
    misfit,
    total,
    load_sem,
    send_sem,
    recv_sem,
):
    shots, rows, depth, width = prev.shape
    here = lax.axis_index("dom")
    left = jnp.maximum(here - 1, 0)
    right = jnp.minimum(here + 1, doms - 1)
    has_left = here > 0
    has_right = here < doms - 1
    chunk = 8
    chunks = rows // chunk
    high_start = rows + MARGIN

    loads = [
        pltpu.make_async_copy(now_hbm, ext.at[0, :, pl.ds(MARGIN, rows)], load_sem.at[0]),
        pltpu.make_async_copy(speed_hbm, speed, load_sem.at[1]),
        pltpu.make_async_copy(prev_hbm, prev, load_sem.at[2]),
        pltpu.make_async_copy(adj_hbm, ext.at[STEPS, :, pl.ds(MARGIN, rows)], load_sem.at[3]),
        pltpu.make_async_copy(later_hbm, later, load_sem.at[4]),
    ]
    for load in loads:
        load.start()

    barrier = pltpu.get_barrier_semaphore()

    @pl.when(has_left)
    def _():
        pl.semaphore_signal(barrier, inc=1, device_id={"dom": left}, device_id_type=MESH)

    @pl.when(has_right)
    def _():
        pl.semaphore_signal(barrier, inc=1, device_id={"dom": right}, device_id_type=MESH)

    pl.semaphore_wait(barrier, has_left.astype(jnp.int32) + has_right.astype(jnp.int32))

    def halo_copies(slot, source):
        base = MARGIN if source is None else 0
        field = ext.at[slot] if source is None else source
        to_left = pltpu.make_async_remote_copy(
            src_ref=field.at[:, pl.ds(base, MARGIN)],
            dst_ref=ext.at[slot, :, pl.ds(high_start, MARGIN)],
            send_sem=send_sem.at[slot, 0],
            recv_sem=recv_sem.at[slot, 1],
            device_id={"dom": left},
            device_id_type=MESH,
        )
        to_right = pltpu.make_async_remote_copy(
            src_ref=field.at[:, pl.ds(base + rows - MARGIN, MARGIN)],
            dst_ref=ext.at[slot, :, pl.ds(0, MARGIN)],
            send_sem=send_sem.at[slot, 1],
            recv_sem=recv_sem.at[slot, 0],
            device_id={"dom": right},
            device_id_type=MESH,
        )
        return to_left, to_right

    copies = [
        halo_copies(slot, {0: now_hbm, STEPS: adj_hbm}.get(slot)) for slot in range(2 * STEPS)
    ]

    def send(slot):
        @pl.when(has_left)
        def _():
            copies[slot][0].start()

        @pl.when(has_right)
        def _():
            copies[slot][1].start()

    def receive(slot):
        @pl.when(has_left)
        def _():
            copies[slot][1].wait_recv()

        @pl.when(has_right)
        def _():
            copies[slot][0].wait_recv()

    send(0)
    send(STEPS)

    edge = jnp.zeros((2 * STEPS, shots, MARGIN, depth, width), jnp.float32)

    @pl.when(jnp.logical_not(has_left))
    def _():
        ext[pl.ds(0, 2 * STEPS), :, pl.ds(0, MARGIN)] = edge

    @pl.when(jnp.logical_not(has_right))
    def _():
        ext[pl.ds(0, 2 * STEPS), :, pl.ds(high_start, MARGIN)] = edge

    lanes = lax.broadcasted_iota(jnp.int32, (depth, width), 1)
    levels = lax.broadcasted_iota(jnp.int32, (depth, width), 0)

    span = chunk * depth
    receivers = rec_lane.shape[2]
    sources = src_lane.shape[2]
    for s in range(shots):
        hot[s] = (
            lax.broadcasted_iota(jnp.int32, (receivers, width), 1) == rec_col[s, :, 1:2]
        ).astype(jnp.float32)
        tall = (
            lax.broadcasted_iota(jnp.int32, (sources, width), 1) == src_col[s]
        ).astype(jnp.float32) * signs[s]
        tall = tall.astype(jnp.bfloat16)

        @pl.loop(0, chunks)
        def _(c):
            cell = lax.broadcasted_iota(jnp.int32, (receivers, span), 1) + c * span
            pick[s, c] = (cell == rec_col[s, :, 0:1]).astype(jnp.float32).astype(jnp.bfloat16)
            cell = lax.broadcasted_iota(jnp.int32, (span, receivers), 0) + c * span
            put[s, c] = (cell == rec_lane[s]).astype(jnp.float32).astype(jnp.bfloat16)
            cell = lax.broadcasted_iota(jnp.int32, (span, sources), 0) + c * span
            wide = (cell == src_lane[s]).astype(jnp.float32).astype(jnp.bfloat16)
            spots = jnp.dot(wide, tall, preferred_element_type=jnp.float32)
            spread_src[s, pl.ds(c * chunk, chunk)] = spots.reshape(chunk, depth, width)

    def laplacian(slot, s, x):
        middle = ext[slot, s, x + MARGIN]
        summed = 3.0 * COEFFS[0] * middle
        for r in range(1, MARGIN + 1):
            beside = ext[slot, s, x + MARGIN + r] + ext[slot, s, x + MARGIN - r]
            beside += jnp.where(levels < depth - r, pltpu.roll(middle, depth - r, 0), 0.0)
            beside += jnp.where(levels >= r, pltpu.roll(middle, r, 0), 0.0)
            beside += jnp.where(lanes < width - r, pltpu.roll(middle, width - r, 1), 0.0)
            beside += jnp.where(lanes >= r, pltpu.roll(middle, r, 1), 0.0)
            summed += COEFFS[r] * beside
        return middle, summed

    def forward(moment, first, last):
        @pl.loop(first, last)
        def _(x):
            squared = COURANT * speed[x] * speed[x]
            for s in range(shots):
                middle, summed = laplacian(moment, s, x)
                before = prev[s, x] if moment == 0 else ext[moment - 1, s, x + MARGIN]
                laps[moment, s, x] = summed
                slot = moment + 1 if moment + 1 < STEPS else 2 * STEPS
                ext[slot, s, x + MARGIN] = (
                    2.0 * middle - before + squared * summed + pulse[s, moment] * spread_src[s, x]
                )

    def backward(moment, first, last):
        slot = 2 * STEPS - moment

        @pl.loop(first, last)
        def _(x):
            squared = COURANT * speed[x] * speed[x]
            gathered = None
            for s in range(shots):
                middle, summed = laplacian(slot, s, x)
                after = later[s, x] if moment == STEPS else ext[slot - 1, s, x + MARGIN]
                earlier = 2.0 * middle - after + squared * summed + landed[moment - 1, s, x]
                if moment > 1:
                    ext[slot + 1, s, x + MARGIN] = earlier
                term = earlier * laps[moment - 1, s, x]
                gathered = term if gathered is None else gathered + term
            if moment < STEPS:
                gathered = gathered + total[x]
            if moment > 1:
                total[x] = gathered
            else:
                out[x] = 2.0 * COURANT * speed[x] * gathered

    def receivers_at(moment):
        slot = moment if moment < STEPS else 2 * STEPS
        for s in range(shots):
            @pl.loop(0, chunks)
            def _(c):
                block = ext[slot, s, pl.ds(MARGIN + c * chunk, chunk)].reshape(span, width)
                part = jnp.dot(pick[s, c], split_two(block), preferred_element_type=jnp.float32)

                @pl.when(c == 0)
                def _():
                    misfit[...] = part

                @pl.when(c > 0)
                def _():
                    misfit[...] += part

            found = misfit[:, :width] + misfit[:, width:]
            sample = jnp.sum(found * hot[s], axis=1, keepdims=True)
            miss = sample - observed[s, :, moment - 1 : moment]
            values = split_two(miss * hot[s])

            @pl.loop(0, chunks)
            def _(c):
                both = jnp.dot(put[s, c], values, preferred_element_type=jnp.float32)
                landed[moment - 1, s, pl.ds(c * chunk, chunk)] = (
                    both[:, :width] + both[:, width:]
                ).reshape(chunk, depth, width)

    for load in loads[:3]:
        load.wait()
    forward(0, MARGIN, rows - MARGIN)
    receive(0)
    forward(0, 0, MARGIN)
    forward(0, rows - MARGIN, rows)
    send(1)
    receivers_at(1)
    for moment in range(1, STEPS):
        receive(moment)
        forward(moment, 0, MARGIN)
        forward(moment, rows - MARGIN, rows)
        if moment + 1 < STEPS:
            send(moment + 1)
        forward(moment, MARGIN, rows - MARGIN)
        receivers_at(moment + 1)
    for load in loads[3:]:
        load.wait()
    for moment in range(STEPS, 0, -1):
        slot = 2 * STEPS - moment
        receive(slot)
        backward(moment, 0, MARGIN)
        backward(moment, rows - MARGIN, rows)
        if moment > 1:
            send(slot + 1)
        backward(moment, MARGIN, rows - MARGIN)
    for slot in range(2 * STEPS):
        @pl.when(has_left)
        def _():
            copies[slot][0].wait_send()

        @pl.when(has_right)
        def _():
            copies[slot][1].wait_send()


def shot_gradient(
    velocity, prev, now, later, adjoint, wavelet, source_cells, signs, record_cells, observed
):
    shots, rows, depth, width = now.shape
    first = lax.axis_index("dom") * rows * depth
    receivers = record_cells.shape[1]
    padding = (-source_cells.shape[1]) % 128
    pad = ((0, 0), (0, padding))
    rec_rows = record_cells // width - first
    rec_col = jnp.stack([rec_rows, record_cells % width], axis=-1)
    src_rows = jnp.pad(source_cells // width - first, pad, constant_values=-1)
    src_lanes = jnp.pad(source_cells % width, pad)
    amplitude = jnp.pad((2 * signs - 1).astype(jnp.float32), pad)
    count = src_rows.shape[1]
    chunk = 8
    span = chunk * depth
    hbm = pl.BlockSpec(memory_space=pl.ANY)
    vmem = pl.BlockSpec(memory_space=pltpu.VMEM)
    smem = pl.BlockSpec(memory_space=pltpu.SMEM)
    f32 = jnp.float32
    return pl.pallas_call(
        functools.partial(wave_kernel, lax.axis_size("dom")),
        out_shape=jax.ShapeDtypeStruct((rows, depth, width), f32),
        in_specs=[hbm] * 5 + [smem] + [vmem] * 6,
        out_specs=vmem,
        scratch_shapes=[
            pltpu.VMEM((2 * STEPS + 1, shots, rows + 2 * MARGIN, depth, width), f32),
            pltpu.VMEM((shots, rows, depth, width), f32),
            pltpu.VMEM((shots, rows, depth, width), f32),
            pltpu.VMEM((rows, depth, width), f32),
            pltpu.VMEM((STEPS, shots, rows, depth, width), f32),
            pltpu.VMEM((shots, rows, depth, width), f32),
            pltpu.VMEM((STEPS, shots, rows, depth, width), f32),
            pltpu.VMEM((shots, rows // chunk, receivers, span), jnp.bfloat16),
            pltpu.VMEM((shots, rows // chunk, span, receivers), jnp.bfloat16),
            pltpu.VMEM((shots, receivers, width), f32),
            pltpu.VMEM((receivers, 2 * width), f32),
            pltpu.VMEM((rows, depth, width), f32),
            pltpu.SemaphoreType.DMA((5,)),
            pltpu.SemaphoreType.DMA((2 * STEPS, 2)),
            pltpu.SemaphoreType.DMA((2 * STEPS, 2)),
        ],
        compiler_params=pltpu.CompilerParams(
            collective_id=0, has_side_effects=True, vmem_limit_bytes=56 * 1024 * 1024
        ),
    )(
        now,
        adjoint,
        prev,
        later,
        velocity,
        wavelet,
        rec_col,
        rec_rows[:, None, :],
        src_lanes[:, :, None],
        src_rows[:, None, :],
        amplitude[:, :, None],
        jnp.swapaxes(observed, 1, 2),
    )


def cosine_basis(length):
    wave_index = jnp.arange(length, dtype=jnp.int32)[:, None]
    position = jnp.arange(length, dtype=jnp.int32)[None, :]
    phase = wave_index * (2 * position + 1) % (4 * length)
    angle = math.pi / (2.0 * length) * phase.astype(jnp.float32)
    factor = jnp.where(wave_index == 0, math.sqrt(1.0 / length), math.sqrt(2.0 / length)).astype(
        jnp.float32
    )
    return factor * jnp.cos(angle)


def prior_gain(length, cutoff):
    scaled = jnp.arange(length, dtype=jnp.float32) / float(cutoff)
    return 1.0 / jnp.sqrt(1.0 + scaled)


def precondition(gradient, noise_cols, rate):
    length = gradient.shape[0]
    basis = cosine_basis(length)
    spectrum = prior_gain(length, length // 32)[:, None]
    highest = lax.Precision.HIGHEST
    grad_hat = jnp.dot(basis, gradient.reshape(length, -1), precision=highest)
    noise_hat = jnp.dot(basis, noise_cols.reshape(length, -1), precision=highest)
    weights = spectrum * (-0.5 * rate * spectrum * grad_hat + jnp.sqrt(rate) * noise_hat)
    update = lax.dot_general(basis, weights, (((0,), (0,)), ((), ())), precision=highest)
    return update.reshape(gradient.shape)


def body(
    velocity,
    noise_field,
    step_size,
    field_prev,
    field_now,
    adjoint_next,
    adjoint_now,
    wavelet,
    source_cells,
    source_signs,
    record_cells,
    observed,
):
    partial_value = shot_gradient(
        velocity,
        field_prev,
        field_now,
        adjoint_next,
        adjoint_now,
        wavelet,
        source_cells,
        source_signs,
        record_cells,
        observed,
    )
    rate = step_size[0]
    shot_rows = velocity.shape[2] // lax.axis_size("shot")
    start = lax.axis_index("shot") * shot_rows
    share = lax.psum_scatter(partial_value, "shot", scatter_dimension=2, tiled=True)
    noise_part = lax.dynamic_slice_in_dim(noise_field, start, shot_rows, 2)
    grad_cols, noise_cols = (
        lax.all_to_all(share, "dom", split_axis=2, concat_axis=0, tiled=True),
        lax.all_to_all(noise_part, "dom", split_axis=2, concat_axis=0, tiled=True),
    )
    update = precondition(grad_cols, noise_cols, rate)
    returned = lax.all_to_all(update, "dom", split_axis=0, concat_axis=2, tiled=True)
    result = lax.dynamic_slice_in_dim(velocity, start, shot_rows, 2) + returned
    return result


def solution(mesh):
    placed = (
        P("dom", None, None),
        P("dom", None, None),
        P(),
        P("shot", "dom", None, None),
        P("shot", "dom", None, None),
        P("shot", "dom", None, None),
        P("shot", "dom", None, None),
        P("shot", None),
        P("shot", None),
        P("shot", None),
        P("shot", None),
        P("shot", None, None),
    )
    return jax.shard_map(
        body, mesh=mesh, in_specs=placed, out_specs=P("dom", None, "shot"), check_vma=False
    )
```

time: 470 us -> 143 us (0.30); the launches traced: 463 us -> 143 us
  other arithmetic: 258 us -> 4.96 us
  local copies, waits for them, and re-layouts: 92.2 us -> 18.8 us
  Pallas kernels: 0 us -> 55.8 us
  starting transfers between devices: 62.2 us -> 14.8 us
    scatter-add x8 -> x0, other arithmetic: 151 us -> none  [place(): flat.at[rows_full, target].add(values, mode='drop').reshape(field.shape)]
    add x8 -> x0, other arithmetic: 78.4 us -> none  [the longest x4 47 us: body(): advanced = 2.0 * current - prior + speed_sq * spread]
    pallas_call x0 -> x1, Pallas kernels: none -> 55.8 us  [shot_gradient(): pl.pallas_call(functools.partial(wave_kernel, lax.axis_size('dom')), out_...]
    ppermute x16 -> x0, starting transfers between devices: 47.2 us -> none  [the longest x8 35.9 us: extended(): lax.ppermute(lax.slice_in_dim(block, block.shape[dim] - width, None, axis...]
    unnamed x133 -> x17, local copies, waits for them, and re-layouts: 50.7 us -> 11.6 us
    gather x8 -> x0, local copies, waits for them, and re-layouts: 23.5 us -> none  [body(): jnp.take_along_axis(advanced.reshape(shots_here, -1), record_clip, axis=1)]
    concatenate x9 -> x0, other arithmetic: 17.6 us -> none  [the longest x8 16.9 us: extended(): block = jnp.concatenate([low, block, high], axis=dim)]
    concatenate x9 -> x0, local copies, waits for them, and re-layouts: 6.44 us -> none  [the longest x8 6.36 us: extended(): block = jnp.concatenate([low, block, high], axis=dim)]
  transfers between devices with their start and end apart: 20 -> 4, of which waited for: 4 -> 3; matrix products, arithmetic and copies ran while one was open for 17% -> 5% of each run, Pallas kernels for 0% -> 0%
where the time goes in v1:
time: 143 us
  Pallas kernels  55.8 us (39%)
  waiting for transfers between devices  29.9 us (21%)
  local copies, waits for them, and re-layouts  18.8 us (13%)
  starting transfers between devices  14.8 us (10%)
  between operations  14.3 us (10%)
  other arithmetic  4.96 us (3%)
  matrix products  4.01 us (3%)
    pallas_call x1, Pallas kernels, shot_gradient(): pl.pallas_call(functools.partial(wave_kernel, lax.axis_size('dom')), out_...  55.8 us
    unnamed x2, waiting for transfers between devices  19.9 us
    unnamed x17, local copies, waits for them, and re-layouts  11.6 us
    all_to_all x1, starting transfers between devices, body(): lax.all_to_all(noise_part, 'dom', split_axis=2, concat_axis=0, tiled=True)  6.77 us
    all_to_all x1, waiting for transfers between devices, body(): lax.all_to_all(update, 'dom', split_axis=0, concat_axis=2, tiled=True)  6.22 us
    all_to_all x1, starting transfers between devices, body(): lax.all_to_all(share, 'dom', split_axis=2, concat_axis=0, tiled=True)  4.61 us
    all_to_all x1, waiting for transfers between devices, body(): lax.all_to_all(share, 'dom', split_axis=2, concat_axis=0, tiled=True)  3.73 us
    all_to_all x1, starting transfers between devices, body(): lax.all_to_all(update, 'dom', split_axis=0, concat_axis=2, tiled=True)  3.37 us
  transfers between devices with their start and end apart: 4, of which 3 were waited for; matrix products, arithmetic and copies ran while one was open for 5% of the time, Pallas kernels for 0%

profile of v1, /device:TPU:0, one launch (start us, length us, event | category | flops | bytes accessed | tf_op | source)
XLA Modules:
  0.0 142.5 jit_solution(7886993211600741604)
XLA Ops:
  6.5 0.0 reduce-scatter.4.cloned.1.call-start
  6.5 0.7 fusion.15
  7.2 0.6 broadcast_in_dim.25.rec_lane
  7.8 0.9 copy.42.rec_col
  8.7 0.7 fusion.16
  9.4 0.8 copy.43.src_col
  10.2 1.5 %copy.41 = f32[2,4,256]{1,2,0:T(8,128)} copy(f32[2,4,256]{2,1,0:T(4,128)} %param.23) | data formatting | bytes 16384 | tf_op args[11]
  11.7 0.7 add_convert_fusion
  12.4 0.8 copy.44.signs
  13.2 0.6 pad.12
  13.8 55.8 %shard_map.118 = f32[32,32,128]{2,1,0:T(8,128)} custom-call(f32[2,32,32,128]{3,2,1,0:T(8,128)} %now_hbm.1, f32[2,32,32,128]{3,2,1,0:T(8,128)} %adj_hbm.1, f32[2,32,32,128]{3,2,1,0:T(8,128)} %prev_hbm.1, f32[2,32,32,128]{3,2,1,0:T(8,128)} %later_hbm.1, f32[32,32,128]{2,1,0:T(8,128)} %speed_hbm.1, f32[2,4]{1,0:T(2,128)} %pulse.1, s32[2,256,2]{2,1,0:T(8,128)} %copy.42.rec_col, ...), custom_call_target="tpu_custom_call" | custom-call | tf_op jit(solution)/shard_map/pallas_call | solution.py:304
  69.6 2.9 %copy.55 = f32[32,32,128]{1,0,2:T(8,128)S(1)} copy(f32[32,32,128]{2,1,0:T(8,128)} %shard_map.118) | data formatting | bytes 1048576
  72.4 0.0 copy-start
  72.5 0.0 copy-start.1
  72.5 1.8 %reshape.41 = f32[128,1024]{1,0:T(8,128)} reshape(f32[128,32,32]{2,1,0:T(8,128)S(1)} %bitcast.46) | data formatting | bytes 1048576
  74.2 0.0 reduce-scatter.4.cloned.1.call-update
  74.3 0.3 constant_dynamic-slice_fusion
  74.6 0.5 copy.58
  75.1 0.9 reshape.45
  76.0 6.8 %all-to-all-start.1 = ((f32[8,1,4096]{2,1,0:T(1,128)}), f32[8,1,4096]{2,1,0:T(1,128)S(1)}, u32[]{:S(2)}, u32[]{:S(2)}) async-start(f32[8,1,4096]{2,1,0:T(1,128)} %reshape.45), calls=%async_computation.1 | async-start | bytes 262144 | tf_op jit(solution)/shard_map/all_to_all | solution.py:406
  82.7 19.9 %reduce-scatter.4.cloned.1.call-done = f32[32,1024]{1,0:T(8,128)} async-done(((f32[128,1024]{1,0:T(8,128)}), f32[32,1024]{1,0:T(8,128)}) %reduce-scatter.4.cloned.1.call-update) | async-done | bytes 131088
  102.6 1.1 reshape.42
  103.8 0.9 reshape.43
  104.7 0.0 all-to-all-done.1
  104.7 4.6 %all-to-all-start = ((f32[8,1,4096]{2,1,0:T(1,128)}), f32[8,1,4096]{2,1,0:T(1,128)S(1)}, u32[]{:S(2)}, u32[]{:S(2)}) async-start(f32[8,1,4096]{2,1,0:T(1,128)} %reshape.43), calls=%async_computation | async-start | bytes 262144 | tf_op jit(solution)/shard_map/all_to_all | solution.py:405
  110.0 0.5 broadcast.157
  110.5 0.9 reduce.1
  111.5 0.2 reshape.46
  111.6 0.5 copy.48
  112.1 0.2 reshape.39
  112.3 3.7 %all-to-all-done = f32[8,1,4096]{2,1,0:T(1,128)S(1)} async-done(((f32[8,1,4096]{2,1,0:T(1,128)}), f32[8,1,4096]{2,1,0:T(1,128)S(1)}, u32[]{:S(2)}, u32[]{:S(2)}) %all-to-all-start) | async-done | bytes 131104 | tf_op jit(solution)/shard_map/all_to_all | solution.py:405
  116.0 0.9 reduce
  117.0 0.2 reshape.44
  117.1 0.5 copy.46
  117.6 0.2 reshape.38
  117.8 1.3 convolution_multiply_fusion.1
  119.1 1.3 fusion.1
  120.5 1.3 fusion.10
  121.9 0.2 copy.49
  122.1 1.0 reshape.47
  123.1 3.4 %all-to-all-start.2 = ((f32[8,1,4096]{2,1,0:T(1,128)}), f32[8,1,4096]{2,1,0:T(1,128)S(1)}, u32[]{:S(2)}, u32[]{:S(2)}) async-start(f32[8,1,4096]{2,1,0:T(1,128)} %reshape.47), calls=%async_computation.2 | async-start | bytes 262144 | tf_op jit(solution)/shard_map/all_to_all | solution.py:409
  126.5 0.5 copy.57
  127.0 6.2 %all-to-all-done.2 = f32[8,1,4096]{2,1,0:T(1,128)S(1)} async-done(((f32[8,1,4096]{2,1,0:T(1,128)}), f32[8,1,4096]{2,1,0:T(1,128)S(1)}, u32[]{:S(2)}, u32[]{:S(2)}) %all-to-all-start.2) | async-done | bytes 131104 | tf_op jit(solution)/shard_map/all_to_all | solution.py:409
  133.2 0.9 reduce.2
  134.1 0.3 reshape.48
  134.4 0.1 copy.54
  134.5 0.1 bitcast_add_fusion
  134.6 1.1 copy.52
  (10 shorter events, 0.1 us)
Async XLA Ops:
  6.5 96.1 %reduce-scatter.4.cloned.1.call-start = ((), (), s32[]{:S(2)}) async-start(), calls=%async_computation.4 | async-start | bytes 655360
  72.4 1.8 %copy-start = (f32[32,32,128]{2,1,0:T(8,128)S(1)}, f32[32,32,128]{2,1,0:T(8,128)}, u32[]{:S(2)}) copy-start(f32[32,32,128]{2,1,0:T(8,128)} %speed_hbm.1) | copy-start | bytes 1572868
  72.5 1.8 %copy-start.1 = (f32[32,32,128]{2,1,0:T(8,128)S(1)}, f32[32,32,128]{2,1,0:T(8,128)}, u32[]{:S(2)}) copy-start(f32[32,32,128]{2,1,0:T(8,128)} %param.13) | copy-start | bytes 1572868
  76.0 28.7 %all-to-all-start.1 = ((f32[8,1,4096]{2,1,0:T(1,128)}), f32[8,1,4096]{2,1,0:T(1,128)S(1)}, u32[]{:S(2)}, u32[]{:S(2)}) async-start(f32[8,1,4096]{2,1,0:T(1,128)} %reshape.45), calls=%async_computation.1 | async-start | bytes 262144 | tf_op jit(solution)/shard_map/all_to_all | solution.py:406
  104.7 11.4 %all-to-all-start = ((f32[8,1,4096]{2,1,0:T(1,128)}), f32[8,1,4096]{2,1,0:T(1,128)S(1)}, u32[]{:S(2)}, u32[]{:S(2)}) async-start(f32[8,1,4096]{2,1,0:T(1,128)} %reshape.43), calls=%async_computation | async-start | bytes 262144 | tf_op jit(solution)/shard_map/all_to_all | solution.py:405
  123.1 10.1 %all-to-all-start.2 = ((f32[8,1,4096]{2,1,0:T(1,128)}), f32[8,1,4096]{2,1,0:T(1,128)S(1)}, u32[]{:S(2)}, u32[]{:S(2)}) async-start(f32[8,1,4096]{2,1,0:T(1,128)} %reshape.47), calls=%async_computation.2 | async-start | bytes 262144 | tf_op jit(solution)/shard_map/all_to_all | solution.py:409
Sparse Core Ops, SparseCore 0:
  74.4 28.2 reduce-scatter.3

commit v2 on v1

--- a/solution.py
+++ b/solution.py
@@ -3,6 +3,7 @@
 
 import jax
 import jax.numpy as jnp
+import numpy as np
 from jax import lax
 from jax.experimental import pallas as pl
 from jax.experimental.pallas import tpu as pltpu
@@ -370,6 +371,197 @@
     return update.reshape(gradient.shape)
 
 
+def shared_kernel(
+    shots,
+    doms,
+    partial,
+    noise,
+    basis,
+    basis_t,
+    gain,
+    step_size,
+    out,
+    folded,
+    noise_fold,
+    sums,
+    own,
+    noise_lines,
+    grad_lines,
+    update,
+    returned,
+    send_sem,
+    recv_sem,
+    shot_send,
+    shot_recv,
+):
+    depth, rows, width = shots * folded.shape[1], folded.shape[2], folded.shape[3]
+    fold = folded.shape[1]
+    lot = fold // doms
+    lane_share = width // shots
+    me = lax.axis_index("shot")
+    here = lax.axis_index("dom")
+    dom_peer = [lax.rem(here + o, doms) for o in range(doms)]
+    shot_peer = [lax.rem(me + o, shots) for o in range(shots)]
+
+    barrier = pltpu.get_barrier_semaphore()
+    for o in range(1, doms):
+        pl.semaphore_signal(barrier, inc=1, device_id={"dom": dom_peer[o]}, device_id_type=MESH)
+    for o in range(1, shots):
+        pl.semaphore_signal(barrier, inc=1, device_id={"shot": shot_peer[o]}, device_id_type=MESH)
+
+    group = lax.broadcasted_iota(jnp.int32, (rows, width), 1) // lane_share
+
+    def fold_lanes(source, target):
+        @pl.loop(0, fold)
+        def _(level):
+            slabs = [
+                source[pl.ds(block * fold + level, rows, stride=depth), :]
+                for block in range(shots)
+            ]
+            for share in range(shots):
+                merged = None
+                for block in range(shots):
+                    shift = (block - share) * lane_share % width
+                    turned = pltpu.roll(slabs[block], shift, 1) if shift else slabs[block]
+                    merged = turned if merged is None else jnp.where(group == block, turned, merged)
+                target[share, level] = merged
+
+    def exchange(phase, source_of, target):
+        moves = []
+        for o in range(1, doms):
+            moves.append(
+                pltpu.make_async_remote_copy(
+                    src_ref=source_of(dom_peer[o]),
+                    dst_ref=target.at[here],
+                    send_sem=send_sem.at[phase, o],
+                    recv_sem=recv_sem.at[phase, o],
+                    device_id={"dom": dom_peer[o]},
+                    device_id_type=MESH,
+                )
+            )
+        return moves
+
+    fold_lanes(partial, folded)
+    pl.semaphore_wait(barrier, doms + shots - 2)
+    sharing = []
+    for o in range(1, shots):
+        move = pltpu.make_async_remote_copy(
+            src_ref=folded.at[shot_peer[o]],
+            dst_ref=sums.at[o],
+            send_sem=shot_send.at[o],
+            recv_sem=shot_recv.at[o],
+            device_id={"shot": shot_peer[o]},
+            device_id_type=MESH,
+        )
+        move.start()
+        sharing.append(move)
+    fold_lanes(noise, noise_fold)
+    noise_moves = exchange(0, lambda d: noise_fold.at[me, pl.ds(d * lot, lot)], noise_lines)
+    for move in noise_moves:
+        move.start()
+    noise_lines[here] = noise_fold[me, pl.ds(here * lot, lot)]
+    for move in noise_moves:
+        move.wait_recv()
+    rate = step_size[0]
+    highest = lax.Precision.HIGHEST
+    lines = doms * rows
+    noise_hats = [
+        jnp.dot(
+            basis[...],
+            noise_lines[:, i].reshape(lines, width),
+            precision=highest,
+            preferred_element_type=jnp.float32,
+        )
+        for i in range(lot)
+    ]
+    root = jnp.sqrt(jnp.full((1, 1), rate, jnp.float32))
+    for move in sharing:
+        move.wait_recv()
+    gathered = folded[me]
+    for o in range(1, shots):
+        gathered = gathered + sums[o]
+    own[...] = gathered
+    grad_moves = exchange(1, lambda d: own.at[pl.ds(d * lot, lot)], grad_lines)
+    for move in grad_moves:
+        move.start()
+    grad_lines[here] = own[pl.ds(here * lot, lot)]
+    for move in grad_moves:
+        move.wait_recv()
+    for i in range(lot):
+        grad_hat = jnp.dot(
+            basis[...],
+            grad_lines[:, i].reshape(lines, width),
+            precision=highest,
+            preferred_element_type=jnp.float32,
+        )
+        weights = gain[...] * (-0.5 * rate * gain[...] * grad_hat + root * noise_hats[i])
+        update[:, i] = jnp.dot(
+            basis_t[...], weights, precision=highest, preferred_element_type=jnp.float32
+        ).reshape(doms, rows, width)
+    back_moves = exchange(2, lambda d: update.at[d], returned)
+    for move in back_moves:
+        move.start()
+    returned[here] = update[here]
+    for move in back_moves:
+        move.wait_recv()
+    for d in range(doms):
+        for i in range(lot):
+            line = returned[d, i]
+            for block in range(shots):
+                shift = -block * lane_share % width
+                turned = pltpu.roll(line, shift, 1) if shift else line
+                out[pl.ds(block * fold + d * lot + i, rows, stride=depth), :] = turned
+    for move in sharing + noise_moves + grad_moves + back_moves:
+        move.wait_send()
+
+
+def shared_update(partial_value, noise_field, step_size):
+    rows, depth, width = partial_value.shape
+    shots, doms = lax.axis_size("shot"), lax.axis_size("dom")
+    length = rows * doms
+    fold = depth // shots
+    lot = fold // doms
+    wave = np.arange(length)[:, None]
+    phase = wave * (2 * np.arange(length)[None, :] + 1) % (4 * length)
+    factor = np.where(wave == 0, math.sqrt(1.0 / length), math.sqrt(2.0 / length))
+    basis = (factor * np.cos(math.pi / (2.0 * length) * phase)).astype(np.float32)
+    gain = (1.0 / np.sqrt(1.0 + wave / (length // 32))).astype(np.float32)
+    f32 = jnp.float32
+    vmem = pl.BlockSpec(memory_space=pltpu.VMEM)
+    smem = pl.BlockSpec(memory_space=pltpu.SMEM)
+    result = pl.pallas_call(
+        functools.partial(shared_kernel, shots, doms),
+        out_shape=jax.ShapeDtypeStruct((rows * depth, width), f32),
+        in_specs=[vmem] * 5 + [smem],
+        out_specs=vmem,
+        scratch_shapes=[
+            pltpu.VMEM((shots, fold, rows, width), f32),
+            pltpu.VMEM((shots, fold, rows, width), f32),
+            pltpu.VMEM((shots, fold, rows, width), f32),
+            pltpu.VMEM((fold, rows, width), f32),
+            pltpu.VMEM((doms, lot, rows, width), f32),
+            pltpu.VMEM((doms, lot, rows, width), f32),
+            pltpu.VMEM((doms, lot, rows, width), f32),
+            pltpu.VMEM((doms, lot, rows, width), f32),
+            pltpu.SemaphoreType.DMA((3, doms)),
+            pltpu.SemaphoreType.DMA((3, doms)),
+            pltpu.SemaphoreType.DMA((shots,)),
+            pltpu.SemaphoreType.DMA((shots,)),
+        ],
+        compiler_params=pltpu.CompilerParams(
+            collective_id=1, has_side_effects=True, vmem_limit_bytes=32 * 1024 * 1024
+        ),
+    )(
+        partial_value.reshape(rows * depth, width),
+        noise_field.reshape(rows * depth, width),
+        jnp.asarray(basis),
+        jnp.asarray(np.ascontiguousarray(basis.T)),
+        jnp.asarray(gain),
+        step_size,
+    )
+    return result.reshape(rows, depth, width)[:, :, : width // shots]
+
+
 def body(
     velocity,
     noise_field,
@@ -399,6 +591,9 @@
     rate = step_size[0]
     shot_rows = velocity.shape[2] // lax.axis_size("shot")
     start = lax.axis_index("shot") * shot_rows
+    if velocity.shape[1] % (lax.axis_size("shot") * lax.axis_size("dom")) == 0:
+        moved = shared_update(partial_value, noise_field, step_size)
+        return lax.dynamic_slice_in_dim(velocity, start, shot_rows, 2) + moved
     share = lax.psum_scatter(partial_value, "shot", scatter_dimension=2, tiled=True)
     noise_part = lax.dynamic_slice_in_dim(noise_field, start, shot_rows, 2)
     grad_cols, noise_cols = (

time: 143 us -> 88.9 us (0.62)
  waiting for transfers between devices: 29.9 us -> 0 us
  Pallas kernels: 55.8 us -> 79.9 us
  starting transfers between devices: 14.8 us -> 0 us
  between operations: 14.3 us -> 0.76 us
  local copies, waits for them, and re-layouts: 18.8 us -> 7.01 us
  matrix products: 4.01 us -> 0 us
  other arithmetic: 4.96 us -> 1.03 us
    pallas_call x0 -> x1, Pallas kernels: none -> 24 us  [shared_update(): pl.pallas_call(functools.partial(shared_kernel, shots, doms), out_shape=j...]
    unnamed x2 -> x0, waiting for transfers between devices: 19.9 us -> none
    all_to_all x3 -> x0, starting transfers between devices: 14.7 us -> none  [the longest x1 6.77 us: body(): lax.all_to_all(noise_part, 'dom', split_axis=2, concat_axis=0, tiled=True)]
    all_to_all x3 -> x0, waiting for transfers between devices: 9.95 us -> none  [the longest x1 6.22 us: body(): lax.all_to_all(update, 'dom', split_axis=0, concat_axis=2, tiled=True)]
    unnamed x17 -> x21, local copies, waits for them, and re-layouts: 11.6 us -> 3.36 us
    dot_general x3 -> x0, matrix products: 4.01 us -> none  [the longest x1 1.34 us: precondition(): lax.dot_general(basis, weights, (((0,), (0,)), ((), ())), precision=highest)]
    all_to_all x3 -> x0, other arithmetic: 2.77 us -> none  [the longest x1 0.92 us: body(): lax.all_to_all(share, 'dom', split_axis=2, concat_axis=0, tiled=True)]
    all_to_all x4 -> x0, local copies, waits for them, and re-layouts: 1.5 us -> none  [the longest x2 0.99 us: body(): lax.all_to_all(share, 'dom', split_axis=2, concat_axis=0, tiled=True)]
  transfers between devices with their start and end apart: 4 -> 0, of which waited for: 3 -> 0; matrix products, arithmetic and copies ran while one was open for 5% -> 0% of each run, Pallas kernels for 0% -> 0%
where the time goes in v2:
time: 88.9 us; the launch traced here: 88.7 us
  Pallas kernels  79.9 us (90%)
  local copies, waits for them, and re-layouts  7.01 us (8%)
  other arithmetic  1.03 us (1%)
    pallas_call x1, Pallas kernels, shot_gradient(): pl.pallas_call(functools.partial(wave_kernel, lax.axis_size('dom')), out_...  55.9 us
    pallas_call x1, Pallas kernels, shared_update(): pl.pallas_call(functools.partial(shared_kernel, shots, doms), out_shape=j...  24 us
    unnamed x21, local copies, waits for them, and re-layouts  3.36 us

profile of v2, /device:TPU:0, one launch (start us, length us, event | category | flops | bytes accessed | tf_op | source)
XLA Modules:
  0.0 88.7 jit_solution(11346512920870987849)
XLA Ops:
  0.0 0.0 copy-start.7
  0.0 0.7 copy-done.7
  0.7 0.9 copy.21.rec_col
  1.6 0.0 copy-start.8
  1.6 0.6 broadcast_in_dim.12.rec_lane
  2.2 0.1 copy-done.8
  2.3 0.0 copy-start.6
  2.3 0.8 copy.22.src_col
  3.1 0.6 pad.12
  3.7 0.0 copy-done.6
  3.7 0.9 copy.20
  4.5 0.0 copy-start.9
  4.5 0.7 copy-done.9
  5.2 0.8 copy.23.signs
  6.0 0.0 copy-start.1
  6.0 0.0 copy-start.2
  6.0 0.0 copy-start.3
  6.0 0.0 copy-start.4
  6.0 55.9 %shard_map.145 = f32[32,32,128]{2,1,0:T(8,128)} custom-call(f32[2,32,32,128]{3,2,1,0:T(8,128)} %now_hbm.1, f32[2,32,32,128]{3,2,1,0:T(8,128)} %adj_hbm.1, f32[2,32,32,128]{3,2,1,0:T(8,128)} %prev_hbm.1, f32[2,32,32,128]{3,2,1,0:T(8,128)} %later_hbm.1, f32[32,32,128]{2,1,0:T(8,128)} %speed_hbm.1, f32[2,4]{1,0:T(2,128)} %pulse.1, s32[2,256,2]{2,1,0:T(8,128)} %copy.21.rec_col, ...), custom_call_target="tpu_custom_call" | custom-call | tf_op jit(solution)/shard_map/pallas_call | solution.py:305
  62.6 0.0 copy-done.1
  62.6 0.0 copy-done.2
  62.6 0.0 copy-done.3
  62.6 0.0 copy-done.4
  62.6 0.0 copy-start
  62.6 1.0 %copy-done = f32[32,32,128]{2,1,0:T(8,128)S(1)} copy-done((f32[32,32,128]{2,1,0:T(8,128)S(1)}, f32[32,32,128]{2,1,0:T(8,128)}, u32[]{:S(2)}) %copy-start) | copy-done | bytes 524312
  63.7 0.0 copy-start.5
  63.7 24.0 %shard_map.146 = f32[1024,128]{1,0:T(8,128)S(1)} custom-call(f32[1024,128]{1,0:T(8,128)S(1)} %bitcast.12, f32[1024,128]{1,0:T(8,128)S(1)} %bitcast.14, f32[256,256]{1,0:T(8,128)S(1)} %copy-done.2, f32[256,256]{1,0:T(8,128)S(1)} %copy-done.3, f32[256,1]{1,0:T(8,128)S(1)} %copy-done.4, f32[1]{0:T(128)S(6)} %copy.24.step_size), custom_call_target="tpu_custom_call" | custom-call | tf_op jit(solution)/shard_map/pallas_call | solution.py:532
  87.7 0.0 copy-done.5
  87.7 1.0 %slice_add_fusion = f32[32,32,32]{2,1,0:T(8,128)} fusion(f32[32,32,128]{2,1,0:T(8,128)S(1)} %bitcast.13, f32[32,32,128]{2,1,0:T(8,128)S(1)} %copy-done.5, s32[]{:T(128)S(6)} %select_n.26), kind=kLoop, calls=%fused_computation | loop fusion | flops 32768 | bytes 393220 | tf_op jit(solution)/shard_map/add | solution.py:596
  (6 shorter events, 0.0 us)
Async XLA Ops:
  0.0 0.7 copy-start.7
  1.6 0.7 copy-start.8
  2.3 1.4 %copy-start.6 = (f32[2,4,256]{2,1,0:T(4,128)S(1)}, f32[2,4,256]{2,1,0:T(4,128)}, u32[]{:S(2)}) copy-start(f32[2,4,256]{2,1,0:T(4,128)} %param.26) | copy-start | bytes 24580
  4.5 0.7 copy-start.9
  6.0 56.6 %copy-start.1 = (f32[32,32,128]{2,1,0:T(8,128)S(1)}, f32[32,32,128]{2,1,0:T(8,128)}, u32[]{:S(2)}) copy-start(f32[32,32,128]{2,1,0:T(8,128)} %param.16) | copy-start | bytes 1572868
  6.0 56.6 %copy-start.2 = (f32[256,256]{1,0:T(8,128)S(1)}, f32[256,256]{1,0:T(8,128)}, u32[]{:S(2)}) copy-start(f32[256,256]{1,0:T(8,128)} %constant.71.clone.basis) | copy-start | bytes 786436
  6.0 56.6 %copy-start.3 = (f32[256,256]{1,0:T(8,128)S(1)}, f32[256,256]{1,0:T(8,128)}, u32[]{:S(2)}) copy-start(f32[256,256]{1,0:T(8,128)} %constant.72.clone.basis_t) | copy-start | bytes 786436
  6.0 56.6 %copy-start.4 = (f32[256,1]{1,0:T(8,128)S(1)}, f32[256,1]{1,0:T(8,128)}, u32[]{:S(2)}) copy-start(f32[256,1]{1,0:T(8,128)} %constant.73.clone.gain) | copy-start | bytes 3076
  62.6 1.0 %copy-start = (f32[32,32,128]{2,1,0:T(8,128)S(1)}, f32[32,32,128]{2,1,0:T(8,128)}, u32[]{:S(2)}) copy-start(f32[32,32,128]{2,1,0:T(8,128)} %shard_map.145) | copy-start | bytes 1572868
  63.7 24.0 %copy-start.5 = (f32[32,32,128]{2,1,0:T(8,128)S(1)}, f32[32,32,128]{2,1,0:T(8,128)}, u32[]{:S(2)}) copy-start(f32[32,32,128]{2,1,0:T(8,128)} %speed_hbm.1) | copy-start | bytes 1572868

commit v3 on v2

--- a/solution.py
+++ b/solution.py
@@ -34,11 +34,9 @@
     later_hbm,
     speed_hbm,
     pulse,
-    rec_col,
-    rec_lane,
-    src_col,
-    src_lane,
-    signs,
+    src_cells,
+    src_signs,
+    record_cells,
     observed,
     out,
     ext,
@@ -51,6 +49,7 @@
     pick,
     put,
     hot,
+    columns,
     misfit,
     total,
     load_sem,
@@ -149,25 +148,50 @@
     levels = lax.broadcasted_iota(jnp.int32, (depth, width), 0)
 
     span = chunk * depth
-    receivers = rec_lane.shape[2]
-    sources = src_lane.shape[2]
+    receivers = record_cells.shape[1]
+    first = here * (rows * depth)
+    row_of = lambda cell: lax.div(cell, jnp.int32(width))
+    lane_of = lambda cell: lax.rem(cell, jnp.int32(width))
+    tile = (width, receivers)
+    place = lax.broadcasted_iota(jnp.int32, tile, 0)
     for s in range(shots):
-        hot[s] = (
-            lax.broadcasted_iota(jnp.int32, (receivers, width), 1) == rec_col[s, :, 1:2]
-        ).astype(jnp.float32)
-        tall = (
-            lax.broadcasted_iota(jnp.int32, (sources, width), 1) == src_col[s]
-        ).astype(jnp.float32) * signs[s]
+        cells = record_cells[s : s + 1, :]
+        rec_rows = row_of(cells) - first
+        table = jnp.where(
+            place == STEPS,
+            jnp.broadcast_to(rec_rows.astype(jnp.float32), tile),
+            jnp.broadcast_to(lane_of(cells).astype(jnp.float32), tile),
+        )
+        for k in range(STEPS):
+            table = jnp.where(place == k, jnp.broadcast_to(observed[s, k : k + 1, :], tile), table)
+        columns[s] = jnp.transpose(table)
+        rec_col = columns[s, :, STEPS : STEPS + 1].astype(jnp.int32)
+        rec_lane = columns[s, :, STEPS + 1 : STEPS + 2].astype(jnp.int32)
+        hot[s] = (lax.broadcasted_iota(jnp.int32, (receivers, width), 1) == rec_lane).astype(
+            jnp.float32
+        )
+        count = src_cells.shape[1]
+        padded = count + (-count) % 128
+        order = lax.broadcasted_iota(jnp.int32, (padded, width), 0)
+        across = lax.broadcasted_iota(jnp.int32, (padded, width), 1)
+        along = lax.broadcasted_iota(jnp.int32, (1, padded), 1)
+        tall = jnp.zeros((padded, width), jnp.float32)
+        src_rows = jnp.full((1, padded), -1, jnp.int32)
+        for j in range(count):
+            cell = src_cells[s, j]
+            sign = (2 * src_signs[s, j] - 1).astype(jnp.float32)
+            tall = jnp.where((order == j) & (across == lane_of(cell)), sign, tall)
+            src_rows = jnp.where(along == j, row_of(cell) - first, src_rows)
         tall = tall.astype(jnp.bfloat16)
 
         @pl.loop(0, chunks)
         def _(c):
             cell = lax.broadcasted_iota(jnp.int32, (receivers, span), 1) + c * span
-            pick[s, c] = (cell == rec_col[s, :, 0:1]).astype(jnp.float32).astype(jnp.bfloat16)
+            pick[s, c] = (cell == rec_col).astype(jnp.float32).astype(jnp.bfloat16)
             cell = lax.broadcasted_iota(jnp.int32, (span, receivers), 0) + c * span
-            put[s, c] = (cell == rec_lane[s]).astype(jnp.float32).astype(jnp.bfloat16)
-            cell = lax.broadcasted_iota(jnp.int32, (span, sources), 0) + c * span
-            wide = (cell == src_lane[s]).astype(jnp.float32).astype(jnp.bfloat16)
+            put[s, c] = (cell == rec_rows).astype(jnp.float32).astype(jnp.bfloat16)
+            cell = lax.broadcasted_iota(jnp.int32, (span, padded), 0) + c * span
+            wide = (cell == src_rows).astype(jnp.float32).astype(jnp.bfloat16)
             spots = jnp.dot(wide, tall, preferred_element_type=jnp.float32)
             spread_src[s, pl.ds(c * chunk, chunk)] = spots.reshape(chunk, depth, width)
 
@@ -184,7 +208,7 @@
         return middle, summed
 
     def forward(moment, first, last):
-        @pl.loop(first, last)
+        @pl.loop(first, last, unroll=MARGIN)
         def _(x):
             squared = COURANT * speed[x] * speed[x]
             for s in range(shots):
@@ -199,7 +223,7 @@
     def backward(moment, first, last):
         slot = 2 * STEPS - moment
 
-        @pl.loop(first, last)
+        @pl.loop(first, last, unroll=MARGIN)
         def _(x):
             squared = COURANT * speed[x] * speed[x]
             gathered = None
@@ -236,7 +260,7 @@
 
             found = misfit[:, :width] + misfit[:, width:]
             sample = jnp.sum(found * hot[s], axis=1, keepdims=True)
-            miss = sample - observed[s, :, moment - 1 : moment]
+            miss = sample - columns[s, :, moment - 1 : moment]
             values = split_two(miss * hot[s])
 
             @pl.loop(0, chunks)
@@ -286,16 +310,7 @@
     velocity, prev, now, later, adjoint, wavelet, source_cells, signs, record_cells, observed
 ):
     shots, rows, depth, width = now.shape
-    first = lax.axis_index("dom") * rows * depth
     receivers = record_cells.shape[1]
-    padding = (-source_cells.shape[1]) % 128
-    pad = ((0, 0), (0, padding))
-    rec_rows = record_cells // width - first
-    rec_col = jnp.stack([rec_rows, record_cells % width], axis=-1)
-    src_rows = jnp.pad(source_cells // width - first, pad, constant_values=-1)
-    src_lanes = jnp.pad(source_cells % width, pad)
-    amplitude = jnp.pad((2 * signs - 1).astype(jnp.float32), pad)
-    count = src_rows.shape[1]
     chunk = 8
     span = chunk * depth
     hbm = pl.BlockSpec(memory_space=pl.ANY)
@@ -305,7 +320,7 @@
     return pl.pallas_call(
         functools.partial(wave_kernel, lax.axis_size("dom")),
         out_shape=jax.ShapeDtypeStruct((rows, depth, width), f32),
-        in_specs=[hbm] * 5 + [smem] + [vmem] * 6,
+        in_specs=[hbm] * 5 + [smem] * 3 + [vmem] * 2,
         out_specs=vmem,
         scratch_shapes=[
             pltpu.VMEM((2 * STEPS + 1, shots, rows + 2 * MARGIN, depth, width), f32),
@@ -317,6 +332,7 @@
             pltpu.VMEM((STEPS, shots, rows, depth, width), f32),
             pltpu.VMEM((shots, rows // chunk, receivers, span), jnp.bfloat16),
             pltpu.VMEM((shots, rows // chunk, span, receivers), jnp.bfloat16),
+            pltpu.VMEM((shots, receivers, width), f32),
             pltpu.VMEM((shots, receivers, width), f32),
             pltpu.VMEM((receivers, 2 * width), f32),
             pltpu.VMEM((rows, depth, width), f32),
@@ -334,12 +350,10 @@
         later,
         velocity,
         wavelet,
-        rec_col,
-        rec_rows[:, None, :],
-        src_lanes[:, :, None],
-        src_rows[:, None, :],
-        amplitude[:, :, None],
-        jnp.swapaxes(observed, 1, 2),
+        source_cells,
+        signs,
+        record_cells,
+        observed,
     )
 
 

time: 88.9 us -> 72 us (0.81)
  Pallas kernels: 79.9 us -> 69 us
  local copies, waits for them, and re-layouts: 7.01 us -> 1.05 us
    pallas_call x1, Pallas kernels: 55.9 us -> 45 us  [shot_gradient(): pl.pallas_call(functools.partial(wave_kernel, lax.axis_size('dom')), out_...]
    unnamed x21 -> x12, local copies, waits for them, and re-layouts: 3.36 us -> 1.05 us
    broadcast_in_dim x5 -> x0, local copies, waits for them, and re-layouts: 2.2 us -> none  [the longest x2 0.81 us: shot_gradient(): src_lanes[:, :, None]]
where the time goes in v3:
time: 72 us; the launch traced here: 71.8 us
  Pallas kernels  69 us (96%)
  local copies, waits for them, and re-layouts  1.05 us (1%)
  other arithmetic  1 us (1%)
  between operations  0.72 us (1%)
    pallas_call x1, Pallas kernels, shot_gradient(): pl.pallas_call(functools.partial(wave_kernel, lax.axis_size('dom')), out_...  45 us
    pallas_call x1, Pallas kernels, shared_update(): pl.pallas_call(functools.partial(shared_kernel, shots, doms), out_shape=j...  24 us

profile of v3, /device:TPU:0, one launch (start us, length us, event | category | flops | bytes accessed | tf_op | source)
XLA Modules:
  0.0 71.8 jit_solution(405286560929962733)
XLA Ops:
  0.0 0.0 copy-start.2
  0.0 0.0 copy-start.3
  0.0 0.0 copy-start.4
  0.0 0.0 copy-start.1
  0.0 45.0 %shard_map.145 = f32[32,32,128]{2,1,0:T(8,128)} custom-call(f32[2,32,32,128]{3,2,1,0:T(8,128)} %now_hbm.1, f32[2,32,32,128]{3,2,1,0:T(8,128)} %adj_hbm.1, f32[2,32,32,128]{3,2,1,0:T(8,128)} %prev_hbm.1, f32[2,32,32,128]{3,2,1,0:T(8,128)} %later_hbm.1, f32[32,32,128]{2,1,0:T(8,128)} %speed_hbm.1, f32[2,4]{1,0:T(2,128)} %pulse.1, s32[2,8]{1,0:T(2,128)} %src_cells.1, ...), custom_call_target="tpu_custom_call" | custom-call | tf_op jit(solution)/shard_map/pallas_call | solution.py:320
  45.7 0.0 copy-done.2
  45.7 0.0 copy-done.3
  45.7 0.0 copy-done.4
  45.7 0.0 copy-done.1
  45.7 0.0 copy-start
  45.8 1.0 %copy-done = f32[32,32,128]{2,1,0:T(8,128)S(1)} copy-done((f32[32,32,128]{2,1,0:T(8,128)S(1)}, f32[32,32,128]{2,1,0:T(8,128)}, u32[]{:S(2)}) %copy-start) | copy-done | bytes 524312
  46.8 0.0 copy-start.5
  46.8 24.0 %shard_map.146 = f32[1024,128]{1,0:T(8,128)S(1)} custom-call(f32[1024,128]{1,0:T(8,128)S(1)} %bitcast.3, f32[1024,128]{1,0:T(8,128)S(1)} %bitcast.5, f32[256,256]{1,0:T(8,128)S(1)} %copy-done.2, f32[256,256]{1,0:T(8,128)S(1)} %copy-done.3, f32[256,1]{1,0:T(8,128)S(1)} %copy-done.4, f32[1]{0:T(128)S(6)} %copy.16.step_size), custom_call_target="tpu_custom_call" | custom-call | tf_op jit(solution)/shard_map/pallas_call | solution.py:546
  70.8 0.0 copy-done.5
  70.8 1.0 %slice_add_fusion = f32[32,32,32]{2,1,0:T(8,128)} fusion(f32[32,32,128]{2,1,0:T(8,128)S(1)} %bitcast.4, f32[32,32,128]{2,1,0:T(8,128)S(1)} %copy-done.5, s32[]{:T(128)S(6)} %select_n.3), kind=kLoop, calls=%fused_computation | loop fusion | flops 32768 | bytes 393220 | tf_op jit(solution)/shard_map/add | solution.py:610
Async XLA Ops:
  0.0 45.7 %copy-start.2 = (f32[256,256]{1,0:T(8,128)S(1)}, f32[256,256]{1,0:T(8,128)}, u32[]{:S(2)}) copy-start(f32[256,256]{1,0:T(8,128)} %constant.17.clone.basis) | copy-start | bytes 786436
  0.0 45.7 %copy-start.3 = (f32[256,256]{1,0:T(8,128)S(1)}, f32[256,256]{1,0:T(8,128)}, u32[]{:S(2)}) copy-start(f32[256,256]{1,0:T(8,128)} %constant.18.clone.basis_t) | copy-start | bytes 786436
  0.0 45.7 %copy-start.4 = (f32[256,1]{1,0:T(8,128)S(1)}, f32[256,1]{1,0:T(8,128)}, u32[]{:S(2)}) copy-start(f32[256,1]{1,0:T(8,128)} %constant.19.clone.gain) | copy-start | bytes 3076
  0.0 45.7 %copy-start.1 = (f32[32,32,128]{2,1,0:T(8,128)S(1)}, f32[32,32,128]{2,1,0:T(8,128)}, u32[]{:S(2)}) copy-start(f32[32,32,128]{2,1,0:T(8,128)} %param.16) | copy-start | bytes 1572868
  45.7 1.0 %copy-start = (f32[32,32,128]{2,1,0:T(8,128)S(1)}, f32[32,32,128]{2,1,0:T(8,128)}, u32[]{:S(2)}) copy-start(f32[32,32,128]{2,1,0:T(8,128)} %shard_map.145) | copy-start | bytes 1572868
  46.8 24.0 %copy-start.5 = (f32[32,32,128]{2,1,0:T(8,128)S(1)}, f32[32,32,128]{2,1,0:T(8,128)}, u32[]{:S(2)}) copy-start(f32[32,32,128]{2,1,0:T(8,128)} %speed_hbm.1) | copy-start | bytes 1572868

commit v4 on v3

--- a/solution.py
+++ b/solution.py
@@ -145,7 +145,7 @@
         ext[pl.ds(0, 2 * STEPS), :, pl.ds(high_start, MARGIN)] = edge
 
     lanes = lax.broadcasted_iota(jnp.int32, (depth, width), 1)
-    levels = lax.broadcasted_iota(jnp.int32, (depth, width), 0)
+    nothing = jnp.zeros((MARGIN, width), jnp.float32)
 
     span = chunk * depth
     receivers = record_cells.shape[1]
@@ -200,8 +200,8 @@
         summed = 3.0 * COEFFS[0] * middle
         for r in range(1, MARGIN + 1):
             beside = ext[slot, s, x + MARGIN + r] + ext[slot, s, x + MARGIN - r]
-            beside += jnp.where(levels < depth - r, pltpu.roll(middle, depth - r, 0), 0.0)
-            beside += jnp.where(levels >= r, pltpu.roll(middle, r, 0), 0.0)
+            beside += jnp.concatenate([middle[r:], nothing[:r]], axis=0)
+            beside += jnp.concatenate([nothing[:r], middle[: depth - r]], axis=0)
             beside += jnp.where(lanes < width - r, pltpu.roll(middle, width - r, 1), 0.0)
             beside += jnp.where(lanes >= r, pltpu.roll(middle, r, 1), 0.0)
             summed += COEFFS[r] * beside

time: 72 us -> 71.6 us (level)
  no operation moved by 1% of the time
where the time goes in v4:
time: 71.6 us; the launch traced here: 71.4 us
  Pallas kernels  68.6 us (96%)
  local copies, waits for them, and re-layouts  1.05 us (1%)
  other arithmetic  1 us (1%)
  between operations  0.72 us (1%)
    pallas_call x1, Pallas kernels, shot_gradient(): pl.pallas_call(functools.partial(wave_kernel, lax.axis_size('dom')), out_...  44.7 us
    pallas_call x1, Pallas kernels, shared_update(): pl.pallas_call(functools.partial(shared_kernel, shots, doms), out_shape=j...  24 us

profile of v4, /device:TPU:0, one launch (start us, length us, event | category | flops | bytes accessed | tf_op | source)
XLA Modules:
  0.0 71.4 jit_solution(596443862660503919)
XLA Ops:
  0.0 0.0 copy-start.2
  0.0 0.0 copy-start.3
  0.0 0.0 copy-start.4
  0.0 0.0 copy-start.1
  0.0 44.7 %shard_map.145 = f32[32,32,128]{2,1,0:T(8,128)} custom-call(f32[2,32,32,128]{3,2,1,0:T(8,128)} %now_hbm.1, f32[2,32,32,128]{3,2,1,0:T(8,128)} %adj_hbm.1, f32[2,32,32,128]{3,2,1,0:T(8,128)} %prev_hbm.1, f32[2,32,32,128]{3,2,1,0:T(8,128)} %later_hbm.1, f32[32,32,128]{2,1,0:T(8,128)} %speed_hbm.1, f32[2,4]{1,0:T(2,128)} %pulse.1, s32[2,8]{1,0:T(2,128)} %src_cells.1, ...), custom_call_target="tpu_custom_call" | custom-call | tf_op jit(solution)/shard_map/pallas_call | solution.py:320
  45.3 0.0 copy-done.2
  45.3 0.0 copy-done.3
  45.3 0.0 copy-done.4
  45.4 0.0 copy-done.1
  45.4 0.0 copy-start
  45.4 1.0 %copy-done = f32[32,32,128]{2,1,0:T(8,128)S(1)} copy-done((f32[32,32,128]{2,1,0:T(8,128)S(1)}, f32[32,32,128]{2,1,0:T(8,128)}, u32[]{:S(2)}) %copy-start) | copy-done | bytes 524312
  46.4 0.0 copy-start.5
  46.4 24.0 %shard_map.146 = f32[1024,128]{1,0:T(8,128)S(1)} custom-call(f32[1024,128]{1,0:T(8,128)S(1)} %bitcast.3, f32[1024,128]{1,0:T(8,128)S(1)} %bitcast.5, f32[256,256]{1,0:T(8,128)S(1)} %copy-done.2, f32[256,256]{1,0:T(8,128)S(1)} %copy-done.3, f32[256,1]{1,0:T(8,128)S(1)} %copy-done.4, f32[1]{0:T(128)S(6)} %copy.16.step_size), custom_call_target="tpu_custom_call" | custom-call | tf_op jit(solution)/shard_map/pallas_call | solution.py:546
  70.4 0.0 copy-done.5
  70.4 1.0 %slice_add_fusion = f32[32,32,32]{2,1,0:T(8,128)} fusion(f32[32,32,128]{2,1,0:T(8,128)S(1)} %bitcast.4, f32[32,32,128]{2,1,0:T(8,128)S(1)} %copy-done.5, s32[]{:T(128)S(6)} %select_n.3), kind=kLoop, calls=%fused_computation | loop fusion | flops 32768 | bytes 393220 | tf_op jit(solution)/shard_map/add | solution.py:610
Async XLA Ops:
  0.0 45.3 %copy-start.2 = (f32[256,256]{1,0:T(8,128)S(1)}, f32[256,256]{1,0:T(8,128)}, u32[]{:S(2)}) copy-start(f32[256,256]{1,0:T(8,128)} %constant.17.clone.basis) | copy-start | bytes 786436
  0.0 45.3 %copy-start.3 = (f32[256,256]{1,0:T(8,128)S(1)}, f32[256,256]{1,0:T(8,128)}, u32[]{:S(2)}) copy-start(f32[256,256]{1,0:T(8,128)} %constant.18.clone.basis_t) | copy-start | bytes 786436
  0.0 45.3 %copy-start.4 = (f32[256,1]{1,0:T(8,128)S(1)}, f32[256,1]{1,0:T(8,128)}, u32[]{:S(2)}) copy-start(f32[256,1]{1,0:T(8,128)} %constant.19.clone.gain) | copy-start | bytes 3076
  0.0 45.3 %copy-start.1 = (f32[32,32,128]{2,1,0:T(8,128)S(1)}, f32[32,32,128]{2,1,0:T(8,128)}, u32[]{:S(2)}) copy-start(f32[32,32,128]{2,1,0:T(8,128)} %param.16) | copy-start | bytes 1572868
  45.4 1.0 %copy-start = (f32[32,32,128]{2,1,0:T(8,128)S(1)}, f32[32,32,128]{2,1,0:T(8,128)}, u32[]{:S(2)}) copy-start(f32[32,32,128]{2,1,0:T(8,128)} %shard_map.145) | copy-start | bytes 1572868
  46.4 24.0 %copy-start.5 = (f32[32,32,128]{2,1,0:T(8,128)S(1)}, f32[32,32,128]{2,1,0:T(8,128)}, u32[]{:S(2)}) copy-start(f32[32,32,128]{2,1,0:T(8,128)} %speed_hbm.1) | copy-start | bytes 1572868
